TPU v7x, 256 devices: a whole 4x4x8 slice. The times are simulated.
256 devices in a mesh: dp: 2 (over core), ctx: 32 (over y, z), grp: 4 (over x).
Axes of the slice: x: 4, y: 4, z: 8, core: 2. Of those that a mesh axis runs over, the one named last changes fastest.
Arguments:
- projected: bfloat16 [4, 8192, 3, 4096], P('dp', 'ctx', None, 'grp'), may hold values from -6 to 6
- short_w: float32 [3, 3, 4096], P(None, None, 'grp'), may hold values from -2.5 to 2.5
- medium_h: bfloat16 [256, 128], P('grp'), may hold values from -3 to 3
- out_w: bfloat16 [4096, 4096], P('ctx', 'grp'), may hold values from -0.09375 to 0.09375
- grad_out: bfloat16 [4, 8192, 4096], P('dp', 'ctx', 'grp'), may hold values from -6 to 6
Outputs:
- block_out: bfloat16 [4, 8192, 4096], P('dp', 'ctx', 'grp')
- grad_projected: bfloat16 [4, 8192, 3, 4096], P('dp', 'ctx', None, 'grp')
- filter_grad: float32 [256, 128], P('grp')
- short_grad: float32 [3, 3, 4096], P(None, None, 'grp')
All inputs are finite; a program needn't handle non-finite values.
Results may differ from a plain program's by a relative error of at most 0.0064.
Values may be sent and summed in bfloat16 or wider, within the bound.
A program may use at most 128 MiB of HBM per device.

v0:
```python
import math

import jax
import jax.numpy as jnp
from jax import lax
from jax.sharding import PartitionSpec as P


def from_behind(block, axis, distance):
    devices = range(lax.axis_size(axis))
    route = [(i - distance, i) for i in devices if i - distance in devices]
    return lax.ppermute(block, axis, route)


def windows(padded, block_rows, reach):
    seqs_here = padded.shape[0]
    block_count = (padded.shape[1] - reach) // block_rows
    extended = jnp.pad(padded, ((0, 0), (0, block_rows - reach), (0, 0), (0, 0)))
    leading = extended[:, : block_count * block_rows].reshape(
        seqs_here, block_count, block_rows, padded.shape[2], padded.shape[3]
    )
    second = extended[:, block_rows:].reshape(
        seqs_here, block_count, block_rows, padded.shape[2], padded.shape[3]
    )[:, :, :reach]
    return jnp.concatenate([leading, second], axis=2)


def banded(filters, block_rows):
    groups_here = filters.shape[0]
    tap_count = filters.shape[1]
    line_width = block_rows + tap_count
    padded_line = jnp.concatenate(
        [filters, jnp.zeros((groups_here, block_rows), filters.dtype)], axis=1
    )
    tiled = jnp.broadcast_to(
        padded_line[:, None, :], (groups_here, block_rows, line_width)
    ).reshape(groups_here, block_rows * line_width)
    return tiled[:, : block_rows * (line_width - 1)].reshape(
        groups_here, block_rows, line_width - 1
    )


def band_conv(turned, matrix, block_rows):
    reach = matrix.shape[2] - block_rows
    windowed = windows(turned, block_rows, reach)
    result = jnp.einsum("gtj,sbjcg->sbtcg", matrix, windowed, preferred_element_type=jnp.float32)
    result = jnp.swapaxes(result, 3, 4)
    return result.reshape(
        turned.shape[0], turned.shape[1] - reach, turned.shape[2] * turned.shape[3]
    )


def lag_sums(grad_blocks, windowed, tap_count):
    products = jnp.einsum(
        "sbtcg,sbjcg->gtj", grad_blocks, windowed, preferred_element_type=jnp.float32
    )
    groups_here = products.shape[0]
    block_rows = products.shape[1]
    line_width = products.shape[2]
    flat_rows = jnp.pad(
        products.reshape(groups_here, block_rows * line_width), ((0, 0), (0, block_rows))
    )
    skewed = flat_rows.reshape(groups_here, block_rows, line_width + 1)[:, :, :tap_count]
    return jnp.sum(skewed, axis=1)[:, ::-1]


def featurize(padded, weights):
    short_reach = weights.shape[1] - 1
    row_count = padded.shape[1] - short_reach
    total = None
    for offset in range(weights.shape[1]):
        start = short_reach - offset
        term = weights[:, offset, :] * padded[:, start : start + row_count]
        total = term if total is None else total + term
    return total


def adjoint(padded, weights):
    short_reach = weights.shape[1] - 1
    row_count = padded.shape[1] - short_reach
    total = None
    for offset in range(weights.shape[1]):
        term = weights[:, offset, :] * padded[:, offset : offset + row_count]
        total = term if total is None else total + term
    return total


def short_sums(feature_grad, padded, short_taps):
    row_count = feature_grad.shape[1]
    short_reach = short_taps - 1
    terms = []
    for offset in range(short_taps):
        start = short_reach - offset
        terms.append(jnp.sum(feature_grad * padded[:, start : start + row_count], axis=(0, 1)))
    return jnp.stack(terms, axis=1)


def shards(projected, short_w, medium_h, out_w, grad_out):
    seq_local = projected.shape[0]
    row_count = projected.shape[1]
    chan_local = projected.shape[3]
    tap_count = medium_h.shape[1]
    reach = tap_count - 1
    short_taps = short_w.shape[1]
    short_reach = short_taps - 1
    group_local = medium_h.shape[0]
    group_size = chan_local // group_local
    block_rows = math.gcd(row_count, 128)
    front_rows = from_behind(projected[:, row_count - short_reach :], "ctx", 1)
    padded_input = jnp.concatenate([front_rows, projected], axis=1)
    features = featurize(padded_input.astype(jnp.float32), short_w)
    product = (features[:, :, 1] * features[:, :, 2]).astype(jnp.bfloat16)
    product_front = from_behind(product[:, row_count - reach :], "ctx", 1)
    product_pad = jnp.concatenate([product_front, product], axis=1)
    query = features[:, :, 0]
    keys = features[:, :, 1]
    values = features[:, :, 2]
    product_turned = jnp.swapaxes(
        product_pad.reshape(seq_local, row_count + reach, group_local, group_size), 2, 3
    )
    mixed = band_conv(product_turned, banded(medium_h[:, ::-1], block_rows), block_rows)
    gated = (query * mixed).astype(jnp.bfloat16)
    whole_gated = lax.all_gather(gated, "grp", axis=2, tiled=True)
    flat_gated = whole_gated.reshape(seq_local * row_count, whole_gated.shape[2])
    flat_cotangent = grad_out.reshape(seq_local * row_count, chan_local)
    projected_out = jnp.dot(
        flat_gated,
        lax.all_gather(out_w, "ctx", axis=0, tiled=True),
        preferred_element_type=jnp.float32,
    )
    block_out = projected_out.astype(jnp.bfloat16).reshape(seq_local, row_count, chan_local)
    input_part = lax.dot_general(
        flat_cotangent,
        lax.all_gather(out_w, "ctx", axis=0, tiled=True),
        (((1,), (1,)), ((), ())),
        preferred_element_type=jnp.float32,
    )
    summed = lax.psum_scatter(input_part, "grp", scatter_dimension=1, tiled=True)
    gated_grad = (
        lax.optimization_barrier(summed.astype(jnp.bfloat16))
        .astype(jnp.float32)
        .reshape(seq_local, row_count, chan_local)
    )
    query_grad = gated_grad * mixed
    mix_grad = (gated_grad * query).astype(jnp.bfloat16)
    mix_back = from_behind(mix_grad[:, :reach], "ctx", -1)
    mix_turned = jnp.swapaxes(
        jnp.concatenate([mix_grad, mix_back], axis=1).reshape(
            seq_local, row_count + reach, group_local, group_size
        ),
        2,
        3,
    )
    product_grad = band_conv(mix_turned, banded(medium_h, block_rows), block_rows)
    grad_blocks = jnp.swapaxes(
        mix_grad.reshape(seq_local, row_count // block_rows, block_rows, group_local, group_size),
        3,
        4,
    )
    filter_part = lag_sums(grad_blocks, windows(product_turned, block_rows, reach), tap_count)
    feature_grad = jnp.stack(
        [query_grad, product_grad * values, product_grad * keys], axis=2
    ).astype(jnp.bfloat16)
    grad_back = from_behind(feature_grad[:, :short_reach], "ctx", -1)
    grad_pad = jnp.concatenate([feature_grad, grad_back], axis=1).astype(jnp.float32)
    grad_projected = adjoint(grad_pad, short_w).astype(jnp.bfloat16)
    short_part = short_sums(
        feature_grad.astype(jnp.float32), padded_input.astype(jnp.float32), short_taps
    )
    filter_total, short_total = lax.psum((filter_part, short_part), ("dp", "ctx"))
    seq_total = seq_local * lax.axis_size("dp")
    length_total = row_count * lax.axis_size("ctx")
    filter_grad = filter_total / math.sqrt(seq_total * length_total * group_size)
    short_grad = short_total / math.sqrt(seq_total * length_total)
    return (block_out, grad_projected, filter_grad, short_grad)


def solution(mesh):
    in_specs = (
        P("dp", "ctx", None, "grp"),
        P(None, None, "grp"),
        P("grp", None),
        P("ctx", "grp"),
        P("dp", "ctx", "grp"),
    )
    out_specs = (
        P("dp", "ctx", "grp"),
        P("dp", "ctx", None, "grp"),
        P("grp", None),
        P(None, None, "grp"),
    )
    return jax.shard_map(shards, mesh=mesh, in_specs=in_specs, out_specs=out_specs, check_vma=False)
```

profile of v0, /device:TPU:1, one launch (start us, length us, event | category | flops | bytes accessed | tf_op | source)
XLA Modules:
  0.0 600.7 jit_solution(14814459723128327061)
XLA Ops:
  8.0 103.6 %all-gather.5.cloned.1.call-done = bf16[4096,1024]{1,0:T(8,128)(2,1)} async-done(((bf16[128,1024]{1,0:T(8,128)(2,1)}), bf16[4096,1024]{1,0:T(8,128)(2,1)}) %all-gather.5.cloned.1.call-update) | async-done | bytes 8388624 | tf_op jit(solution)/shard_map/all_gather | solution.py:128
  111.5 10.1 %fusion.31 = f32[512,4096]{1,0:T(8,128)} fusion(bf16[512,1024]{1,0:T(8,128)(2,1)S(1)} %bitcast.91, bf16[4096,1024]{1,0:T(8,128)(2,1)} %all-gather.5.cloned.1.call-done), kind=kOutput, calls=%fused_computation.57 | convolution fusion | flops 4294967296 | bytes 17825792 | tf_op jit(solution)/shard_map/dot_general | solution.py:132
  124.5 4.6 copy.57
  130.0 4.6 maximum_convert_fusion
  138.3 5.9 multiply_add_fusion
  144.2 58.5 %reduce-scatter.2.cloned.1.call-done = f32[512,1024]{1,0:T(8,128)} async-done(((f32[512,4096]{1,0:T(8,128)}), f32[512,1024]{1,0:T(8,128)}) %reduce-scatter.2.cloned.1.call-update) | async-done | bytes 2097168 | tf_op jit(solution)/shard_map/reduce_scatter | solution.py:138
  216.5 15.8 %reshape.121 = bf16[64,128,255,1,1]{2,1,0,3,4:T(8,128)(2,1)} reshape(bf16[64,32640]{1,0:T(8,128)(2,1)} %slice.126) | data formatting | bytes 8355840 | tf_op jit(solution)/shard_map/reshape | solution.py:38
  243.7 4.1 fusion.20
  250.3 3.9 reshape.116
  254.1 5.9 multiply_convert_fusion.1
  262.1 4.8 collective-permute-start.1
  272.2 16.0 %reshape.120 = bf16[64,128,255,1,1]{2,1,0,3,4:T(8,128)(2,1)} reshape(bf16[64,32640]{1,0:T(8,128)(2,1)} %slice.122) | data formatting | bytes 8355840 | tf_op jit(solution)/shard_map/reshape | solution.py:38
  297.5 3.9 fusion.26
  308.1 3.7 fusion.17
  318.7 6.2 %convolution_bitcast_fusion = f32[64,128,255]{2,1,0:T(8,128)} fusion(bf16[2,2,255,16,64]{2,3,1,0,4:T(8,128)(2,1)} %copy-done.5, bf16[2,2,128,16,64]{2,1,0,3,4:T(2,128)(2,1)S(1)} %copy-done.9), kind=kOutput, calls=%fused_computation.20 | convolution fusion | flops 267386880 | bytes 11493376 | tf_op jit(solution)/shard_map/sbtcg,sbjcg->gtj/dot_general | solution.py:54
  324.9 9.2 %reshape.118 = f32[64,32640]{1,0:T(8,128)} reshape(f32[64,128,255]{2,1,0:T(8,128)} %convolution_bitcast_fusion) | data formatting | bytes 16711680 | tf_op jit(solution)/shard_map/reshape | solution.py:61
  334.1 4.0 pad.16
  344.4 10.9 %fusion = (f32[3,1024]{1,0:T(4,128)S(1)}, f32[3,1024]{1,0:T(4,128)S(1)}, f32[3,1024]{1,0:T(4,128)S(1)}) fusion(f32[2,258,3,1024]{1,3,0,2:T(8,128)} %copy-done.2, bf16[2,256,1,1024]{1,3,0,2:T(8,128)(2,1)S(1)} %copy-done.4, bf16[2,256,1,1024]{1,3,0,2:T(8,128)(2,1)S(1)} %copy-done.3, bf16[2,256,1,1024]{1,3,0,2:T(8,128)(2,1)S(1)} %multiply_convert_fusion.2), kind=kLoop, calls=%fused_computation.3 | loop fusion | flops 14146560 | bytes 22056960 | tf_op jit(solution)/shard_map/reduce_sum | solution.py:94
  371.8 5.8 fusion.4
  377.6 4.6 copy.78
  382.2 145.3 %all-reduce.8.cloned.1.call-done = (f32[64,128]{1,0:T(8,128)}, f32[3,3,1024]{2,0,1:T(4,128)}) async-done(((f32[64,128]{1,0:T(8,128)}, f32[3,3,1024]{2,0,1:T(4,128)}), (f32[64,128]{1,0:T(8,128)}, f32[3,3,1024]{2,0,1:T(4,128)})) %all-reduce.8.cloned.1.call-update) | async-done | bytes 69648 | tf_op jit(solution)/shard_map/psum | solution.py:170
  530.4 46.8 %all-gather.3.cloned.1.call-done = bf16[2,256,4096]{1,2,0:T(8,128)(2,1)} async-done(((bf16[2,256,1024]{1,2,0:T(8,128)(2,1)}), bf16[2,256,4096]{1,2,0:T(8,128)(2,1)}) %all-gather.3.cloned.1.call-update) | async-done | bytes 4194320 | tf_op jit(solution)/shard_map/all_gather | solution.py:123
  577.3 6.5 %copy.63 = bf16[2,256,4096]{2,1,0:T(8,128)(2,1)} copy(bf16[2,256,4096]{1,2,0:T(8,128)(2,1)} %all-gather.3.cloned.1.call-done) | data formatting | bytes 8388608 | tf_op jit(solution)/shard_map/all_gather | solution.py:123
  583.8 10.2 %convolution_convert_fusion = bf16[512,1024]{1,0:T(8,128)(2,1)} fusion(bf16[512,4096]{1,0:T(8,128)(2,1)} %bitcast.102, bf16[4096,1024]{1,0:T(8,128)(2,1)} %all-gather.5.cloned.1.call-done), kind=kOutput, calls=%fused_computation.42 | convolution fusion | flops 4295491584 | bytes 13631488 | tf_op jit(solution)/shard_map/dot_general | solution.py:126
  (93 shorter events, 91.3 us)
Async XLA Ops:
  7.2 104.4 %copy-start = (bf16[2,256,1024]{2,1,0:T(8,128)(2,1)S(1)}, bf16[2,256,1024]{2,1,0:T(8,128)(2,1)}, u32[]{:S(2)}) copy-start(bf16[2,256,1024]{2,1,0:T(8,128)(2,1)} %param.9) | copy-start | bytes 3145732
  7.2 104.3 %all-gather.5.cloned.1.call-start = ((), (), s32[]{:S(2)}) async-start(), calls=%async_computation.2 | async-start | bytes 8650752 | tf_op jit(solution)/shard_map/all_gather | solution.py:128
  7.9 194.7 %reduce-scatter.2.cloned.1.call-start = ((), (), s32[]{:S(2)}) async-start(), calls=%async_computation.3 | async-start | bytes 10485760 | tf_op jit(solution)/shard_map/reduce_scatter | solution.py:138
  121.7 2.8 copy-start.11
  121.7 405.9 %all-reduce.8.cloned.1.call-start = ((), (), s32[]{:S(2)}) async-start(), calls=%async_computation.4 | async-start | bytes 163840 | tf_op jit(solution)/shard_map/psum | solution.py:170
  122.7 6.5 %collective-permute-start = (bf16[2,2,3,1024]{3,1,2,0:T(2,128)(2,1)S(1)}, bf16[2,2,3,1024]{3,1,2,0:T(2,128)(2,1)S(1)}, u32[]{:S(2)}, u32[]{:S(2)}) collective-permute-start(bf16[2,2,3,1024]{3,1,2,0:T(2,128)(2,1)S(1)} %slice.89), channel_id=1, source_target_pairs={{0,4},{4,8},{8,12},{12,16},{16,20},{20,24},{24,28},{28,32},{32,36}... | collective-permute-start | bytes 73736 | tf_op jit(solution)/shard_map/ppermute | solution.py:12
  134.6 3.7 copy-start.2
  206.4 4.8 copy-start.10
  208.9 2.4 copy-start.6
  209.8 22.5 %collective-permute-start.2 = (bf16[2,127,1024]{1,2,0:T(8,128)(2,1)}, bf16[2,127,1024]{1,2,0:T(8,128)(2,1)}, u32[]{:S(2)}, u32[]{:S(2)}) collective-permute-start(bf16[2,127,1024]{1,2,0:T(8,128)(2,1)} %slice.123), channel_id=1, source_target_pairs={{4,0},{8,4},{12,8},{16,12},{20,16},{24,20},{28,24},{32,28},{36,32}... | collective-permute-start | bytes 1560584 | tf_op jit(solution)/shard_map/ppermute | solution.py:12
  260.1 1.0 copy-start.7
  262.1 39.3 %collective-permute-start.1 = (bf16[2,127,1024]{1,2,0:T(8,128)(2,1)}, bf16[2,127,1024]{1,2,0:T(8,128)(2,1)}, u32[]{:S(2)}, u32[]{:S(2)}) collective-permute-start(bf16[2,127,1024]{1,2,0:T(8,128)(2,1)} %slice.119), channel_id=1, source_target_pairs={{0,4},{4,8},{8,12},{12,16},{16,20},{20,24},{24,28},{28,32},{32,36}... | collective-permute-start | bytes 1560584 | tf_op jit(solution)/shard_map/ppermute | solution.py:12
  297.5 3.9 copy-start.8
  306.7 1.3 copy-start.5
  315.6 3.0 copy-start.9
  341.2 3.2 copy-start.3
  341.2 3.2 copy-start.4
  355.9 221.4 %all-gather.3.cloned.1.call-start = ((), (), s32[]{:S(2)}) async-start(), calls=%async_computation.1 | async-start | bytes 5242880 | tf_op jit(solution)/shard_map/all_gather | solution.py:123
  362.9 4.6 collective-permute-start.3
  583.8 10.2 %copy-start.1 = (bf16[2,256,1024]{2,1,0:T(8,128)(2,1)S(1)}, bf16[2,256,1024]{2,1,0:T(8,128)(2,1)}, u32[]{:S(2)}) copy-start(bf16[2,256,1024]{2,1,0:T(8,128)(2,1)} %param.9) | copy-start | bytes 3145732
Sparse Core Ops, SparseCore 0:
  10.6 100.9 all-gather.4
  121.8 80.7 reduce-scatter.1
  356.0 171.5 all-reduce.7
  529.8 47.3 all-gather.2
where the time goes:
time: 607 us; the launch traced here: 601 us
  waiting for transfers between devices  358 us (59%)
  local copies, waits for them, and re-layouts  127 us (21%)
  other arithmetic  56.9 us (9%)
  matrix products  34.4 us (6%)
  between operations  14.3 us (2%)
  starting transfers between devices  9.42 us (2%)
    psum x1, waiting for transfers between devices, shards(): lax.psum((filter_part, short_part), ('dp', 'ctx'))  145 us
    all_gather x1, waiting for transfers between devices, shards(): lax.all_gather(out_w, 'ctx', axis=0, tiled=True)  104 us
    reduce_scatter x1, waiting for transfers between devices, shards(): lax.psum_scatter(input_part, 'grp', scatter_dimension=1, tiled=True)  58.5 us
    all_gather x1, waiting for transfers between devices, shards(): whole_gated = lax.all_gather(gated, 'grp', axis=2, tiled=True)  46.8 us
    reshape x2, local copies, waits for them, and re-layouts, banded(): tiled[:, :block_rows * (line_width - 1)]  31.8 us
    unnamed x34, local copies, waits for them, and re-layouts  25.5 us
  transfers between devices with their start and end apart: 8, of which 5 were waited for; matrix products, arithmetic and copies ran while one was open for 16% of the time, Pallas kernels for 0%

commit v1 on v0

v1 whole, which is shorter than its diff:
```python
import functools
import math

import jax
import jax.numpy as jnp
from jax import lax
from jax.experimental import pallas as pl
from jax.experimental.pallas import tpu as pltpu
from jax.sharding import PartitionSpec as P

BF = jnp.bfloat16
F32 = jnp.float32
LANES = 128
BLOCK = 128
HALO = 16
MESH = pl.DeviceIdType.MESH


def from_behind(block, axis, distance):
    devices = range(lax.axis_size(axis))
    route = [(i - distance, i) for i in devices if i - distance in devices]
    return lax.ppermute(block, axis, route)


def fill(scratch, front, rows):
    scratch[0:HALO, :] = front.astype(F32)
    scratch[HALO : HALO + rows.shape[0], :] = rows.astype(F32)


def feature(scratch, taps, stream, count):
    total = None
    for offset in range(taps.shape[1]):
        start = HALO - offset
        term = taps[stream, offset : offset + 1, :] * scratch[start : start + count, :]
        total = term if total is None else total + term
    return total


def band_rows(lines, band):
    groups = lines.shape[0]
    for g in range(groups):
        line = jnp.broadcast_to(lines[g : g + 1, :], (BLOCK, lines.shape[1]))
        turned = pltpu.roll(line, 0, 1, stride=1, stride_axis=0)
        band[g * BLOCK : (g + 1) * BLOCK, :] = turned.astype(BF)


def group_of_lane(shape, groups):
    lane = lax.broadcasted_iota(jnp.int32, shape, len(shape) - 1)
    return (lane % LANES) // (LANES // groups)


def own_group(wide, groups):
    owner = group_of_lane((BLOCK, wide.shape[1]), groups)
    kept = wide[0:BLOCK]
    for g in range(1, groups):
        kept = jnp.where(owner == g, wide[g * BLOCK : (g + 1) * BLOCK], kept)
    return kept


def window_pair(padded, start):
    return jnp.concatenate(
        [padded[s, start : start + 2 * BLOCK, :] for s in range(padded.shape[0])], axis=1
    )


def tail_kernel(front_ref, rows_ref, taps_ref, out_ref, scratch):
    for s in range(rows_ref.shape[0]):
        found = []
        for stream in (1, 2):
            fill(scratch, front_ref[s, stream], rows_ref[s, stream])
            found.append(feature(scratch, taps_ref, stream, BLOCK))
        out_ref[s] = (found[0] * found[1]).astype(BF)


def forward_kernel(
    front_ref, rows_ref, taps_ref, lines_ref, behind_ref,
    gated_ref, mixed_ref, product_ref, scratch, padded, queries, band,
):
    seqs, row_count = rows_ref.shape[0], rows_ref.shape[2]
    groups = lines_ref.shape[0]
    band_rows(lines_ref[...], band)
    for s in range(seqs):
        found = []
        for stream in range(3):
            fill(scratch, front_ref[s, stream], rows_ref[s, stream])
            found.append(feature(scratch, taps_ref, stream, row_count))
        queries[s] = found[0]
        product = (found[1] * found[2]).astype(BF)
        product_ref[s] = product
        padded[s, 0:BLOCK, :] = behind_ref[s]
        padded[s, BLOCK : BLOCK + row_count, :] = product
    for b in range(row_count // BLOCK):
        here = slice(b * BLOCK, (b + 1) * BLOCK)
        wide = jnp.dot(
            band[...], window_pair(padded, b * BLOCK), preferred_element_type=F32
        )
        kept = own_group(wide, groups)
        for s in range(seqs):
            mixed = kept[:, s * LANES : (s + 1) * LANES]
            mixed_ref[s, here, :] = mixed
            gated_ref[s, here, :] = (queries[s, here, :] * mixed).astype(BF)


def mix_kernel(
    cotangent_ref, front_ref, rows_ref, taps_ref, lines_ref, mixed_ref,
    mix_ref, head_ref, scratch, band,
):
    seqs, row_count = rows_ref.shape[0], rows_ref.shape[2]
    groups = lines_ref.shape[0]
    band_rows(lines_ref[...], band)
    for s in range(seqs):
        fill(scratch, front_ref[s, 0], rows_ref[s, 0])
        query = feature(scratch, taps_ref, 0, row_count)
        mix_ref[s] = (cotangent_ref[s].astype(F32) * query).astype(BF)
    wide = jnp.dot(band[...], window_pair(mix_ref, 0), preferred_element_type=F32)
    kept = own_group(wide, groups)
    for s in range(seqs):
        pulled = kept[0:HALO, s * LANES : (s + 1) * LANES]
        found = []
        for stream in (1, 2):
            fill(scratch, front_ref[s, stream], rows_ref[s, stream, 0:HALO])
            found.append(feature(scratch, taps_ref, stream, HALO))
        head_ref[s, 0] = (cotangent_ref[s, 0:HALO, :].astype(F32) * mixed_ref[s, 0:HALO, :]).astype(BF)
        head_ref[s, 1] = (pulled * found[1]).astype(BF)
        head_ref[s, 2] = (pulled * found[0]).astype(BF)


def filter_kernel(mix_ref, product_ref, behind_ref, sums_ref, padded):
    seqs, row_count = product_ref.shape[0], product_ref.shape[1]
    groups = sums_ref.shape[0]
    blocks = row_count // BLOCK
    for s in range(seqs):
        padded[s, 0:BLOCK, :] = behind_ref[s]
        padded[s, BLOCK : BLOCK + row_count, :] = product_ref[s]
    rows = lax.broadcasted_iota(jnp.int32, (BLOCK, BLOCK), 0)
    columns = lax.broadcasted_iota(jnp.int32, (BLOCK, BLOCK), 1)
    upturn = (rows + columns == BLOCK - 1).astype(BF)
    parts, wins = [], []
    for s in range(seqs):
        for b in range(blocks):
            parts.append(mix_ref[s, b * BLOCK : (b + 1) * BLOCK, :])
            wins.append(padded[s, b * BLOCK : (b + 2) * BLOCK, :])
    grads = jnp.dot(upturn, jnp.concatenate(parts, axis=1), preferred_element_type=F32)
    windows = jnp.concatenate(wins, axis=1)
    owner = group_of_lane(grads.shape, groups)
    stacked = jnp.concatenate(
        [jnp.where(owner == g, grads, 0.0).astype(BF) for g in range(groups)], axis=0
    )
    lags = lax.dot_general(
        stacked, windows, (((1,), (1,)), ((), ())), preferred_element_type=F32
    )
    for g in range(groups):
        turned = pltpu.roll(lags[g * BLOCK : (g + 1) * BLOCK], 0, 1, stride=1, stride_axis=0)
        sums_ref[g : g + 1, :] = jnp.sum(turned[:, BLOCK:], axis=0, keepdims=True)


def backward_kernel(
    cotangent_ref, front_ref, rows_ref, taps_ref, lines_ref, mixed_ref,
    mix_ref, ahead_ref, next_ref, grad_ref, short_ref, scratch, padded, pulled, later, band,
):
    seqs, row_count = rows_ref.shape[0], rows_ref.shape[2]
    groups = lines_ref.shape[0]
    taps = taps_ref.shape[1]
    band_rows(lines_ref[...], band)
    for s in range(seqs):
        padded[s, 0:row_count, :] = mix_ref[s]
        padded[s, row_count : row_count + BLOCK, :] = ahead_ref[s]
    for b in range(row_count // BLOCK):
        wide = jnp.dot(
            band[...], window_pair(padded, b * BLOCK), preferred_element_type=F32
        )
        kept = own_group(wide, groups)
        for s in range(seqs):
            pulled[s, b * BLOCK : (b + 1) * BLOCK, :] = kept[:, s * LANES : (s + 1) * LANES]
    short_ref[...] = jnp.zeros_like(short_ref)
    for s in range(seqs):
        for stream in range(3):
            if stream == 0:
                grad = cotangent_ref[s].astype(F32) * mixed_ref[s]
            else:
                other = 3 - stream
                fill(scratch, front_ref[s, other], rows_ref[s, other])
                grad = pulled[s] * feature(scratch, taps_ref, other, row_count)
            grad = grad.astype(BF).astype(F32)
            fill(scratch, front_ref[s, stream], rows_ref[s, stream])
            later[0:row_count, :] = grad
            later[row_count : row_count + HALO, :] = next_ref[s, stream].astype(F32)
            total = None
            for offset in range(taps):
                term = taps_ref[stream, offset : offset + 1, :] * later[offset : offset + row_count, :]
                total = term if total is None else total + term
                at = HALO - offset
                row = stream * taps + offset
                short_ref[0, row : row + 1, :] += jnp.sum(
                    grad * scratch[at : at + row_count, :], axis=0, keepdims=True
                )
            grad_ref[s, stream] = total.astype(BF)


def reduce_kernel(x_ref, o_ref, zbuf, part, ybuf, whole, zs, zr, ys, yr, os, orr):
    pieces = x_ref.shape[0]
    me, core = lax.axis_index("ctx"), lax.axis_index("dp")
    line, place = me // pieces, me % pieces
    lines = lax.axis_size("ctx") // pieces
    peers = lines * 2
    mine = line * 2 + core

    def along(step):
        return {"ctx": line * pieces + (place + step) % pieces}

    def across(step):
        other = (mine + step) % peers
        return {"ctx": (other // 2) * pieces + place, "dp": other % 2}

    barrier = pltpu.get_barrier_semaphore()
    for step in range(1, pieces):
        pl.semaphore_signal(barrier, inc=1, device_id=along(step), device_id_type=MESH)
    for step in range(1, peers):
        pl.semaphore_signal(barrier, inc=1, device_id=across(step), device_id_type=MESH)
    pl.semaphore_wait(barrier, pieces + peers - 2)

    def first(step):
        return pltpu.make_async_remote_copy(
            src_ref=x_ref.at[(place + step) % pieces], dst_ref=zbuf.at[place],
            send_sem=zs.at[step], recv_sem=zr.at[step],
            device_id=along(step), device_id_type=MESH,
        )

    def second(step):
        return pltpu.make_async_remote_copy(
            src_ref=part, dst_ref=ybuf.at[mine], send_sem=ys.at[step], recv_sem=yr.at[step],
            device_id=across(step), device_id_type=MESH,
        )

    def third(step):
        return pltpu.make_async_remote_copy(
            src_ref=whole, dst_ref=o_ref.at[place], send_sem=os.at[step], recv_sem=orr.at[step],
            device_id=along(step), device_id_type=MESH,
        )

    for step in range(1, pieces):
        first(step).start()
    zbuf[place] = x_ref[place]
    for step in range(1, pieces):
        first(step).wait_recv()
    total = zbuf[0]
    for k in range(1, pieces):
        total = total + zbuf[k]
    part[...] = total
    for step in range(1, peers):
        second(step).start()
    ybuf[mine] = total
    for step in range(1, peers):
        second(step).wait_recv()
    total = ybuf[0]
    for k in range(1, peers):
        total = total + ybuf[k]
    whole[...] = total
    for step in range(1, pieces):
        third(step).start()
    o_ref[place] = total
    for step in range(1, pieces):
        third(step).wait_recv()
    for step in range(1, pieces):
        first(step).wait_send()
        third(step).wait_send()
    for step in range(1, peers):
        second(step).wait_send()


def tiled(kernel, ins, outs, scratch, arrays, tiles, flops=0):
    read = sum(math.prod(a.shape) * a.dtype.itemsize for a in arrays)
    return pl.pallas_call(
        kernel,
        grid=(tiles,),
        in_specs=[pl.BlockSpec(block, index) for block, index in ins],
        out_specs=[pl.BlockSpec(block, index) for block, index, _, _ in outs],
        out_shape=[jax.ShapeDtypeStruct(shape, kind) for _, _, shape, kind in outs],
        scratch_shapes=scratch,
        cost_estimate=pl.CostEstimate(flops=flops, bytes_accessed=read, transcendentals=0),
        compiler_params=pltpu.CompilerParams(vmem_limit_bytes=48 << 20),
    )(*arrays)


def shards(projected, short_w, medium_h, out_w, grad_out):
    seqs, row_count, _, chans = projected.shape
    taps = medium_h.shape[1]
    groups_here = medium_h.shape[0]
    tiles = chans // LANES
    groups = groups_here // tiles
    rows = jnp.swapaxes(projected, 1, 2)

    lines_behind = jnp.pad(medium_h[:, ::-1].astype(F32), ((0, 0), (1, 2 * BLOCK - taps - 1)))
    lines_ahead = jnp.pad(medium_h.astype(F32), ((0, 0), (0, 2 * BLOCK - taps)))

    lane3 = lambda i: (0, 0, i)
    lane4 = lambda i: (0, 0, 0, i)
    front_spec = ((seqs, 3, HALO, LANES), lane4)
    rows_spec = ((seqs, 3, row_count, LANES), lane4)
    taps_spec = ((3, short_w.shape[1], LANES), lane3)
    lines_spec = ((groups, 2 * BLOCK), lambda i: (i, 0))
    edge_spec = ((seqs, BLOCK, LANES), lane3)
    full_spec = ((seqs, row_count, LANES), lane3)
    full = (seqs, row_count, chans)
    line_rows = pltpu.VMEM((row_count + HALO, LANES), F32)
    long_rows = pltpu.VMEM((seqs, row_count + BLOCK, LANES), BF)
    bands = pltpu.VMEM((groups * BLOCK, 2 * BLOCK), BF)

    front = from_behind(rows[:, :, row_count - HALO :], "ctx", 1)
    tail = tiled(
        tail_kernel,
        [
            ((seqs, 3, HALO, LANES), lambda i: (0, 0, (row_count - BLOCK) // HALO - 1, i)),
            ((seqs, 3, BLOCK, LANES), lambda i: (0, 0, row_count // BLOCK - 1, i)),
            taps_spec,
        ],
        [(*edge_spec, (seqs, BLOCK, chans), BF)],
        [line_rows],
        (rows, rows, short_w),
        tiles,
    )[0]
    behind = from_behind(tail, "ctx", 1)
    gated, mixed, product = tiled(
        forward_kernel,
        [front_spec, rows_spec, taps_spec, lines_spec, edge_spec],
        [(*full_spec, full, BF), (*full_spec, full, F32), (*full_spec, full, BF)],
        [line_rows, long_rows, pltpu.VMEM((seqs, row_count, LANES), F32), bands],
        (front, rows, short_w, lines_behind, behind),
        tiles,
    )

    whole_w = lax.all_gather(out_w, "ctx", axis=0, tiled=True)
    whole_gated = lax.all_gather(gated, "grp", axis=2, tiled=True)
    flat_gated = whole_gated.reshape(seqs * row_count, whole_gated.shape[2])
    block_out = jnp.dot(flat_gated, whole_w, preferred_element_type=F32).astype(BF).reshape(full)
    input_part = lax.dot_general(
        grad_out.reshape(seqs * row_count, chans), whole_w, (((1,), (1,)), ((), ())), preferred_element_type=F32
    )
    summed = lax.psum_scatter(input_part, "grp", scatter_dimension=1, tiled=True)
    cotangent = summed.astype(BF).reshape(full)

    mix, head = tiled(
        mix_kernel,
        [full_spec, front_spec, rows_spec, taps_spec, lines_spec, full_spec],
        [(*full_spec, full, BF), (*front_spec, (seqs, 3, HALO, chans), BF)],
        [line_rows, bands],
        (cotangent, front, rows, short_w, lines_ahead, mixed),
        tiles,
    )
    ahead = from_behind(mix[:, :BLOCK], "ctx", -1)
    later = from_behind(head, "ctx", -1)
    filter_part = tiled(
        filter_kernel,
        [full_spec, full_spec, edge_spec],
        [((groups, LANES), lambda i: (i, 0), (groups_here, taps), F32)],
        [long_rows],
        (mix, product, behind),
        tiles,
    )[0]
    grad, short_part = tiled(
        backward_kernel,
        [full_spec, front_spec, rows_spec, taps_spec, lines_spec, full_spec, full_spec, edge_spec, front_spec],
        [(*rows_spec, rows.shape, BF), ((1, HALO, LANES), lambda i: (i, 0, 0), (tiles, HALO, LANES), F32)],
        [line_rows, long_rows, pltpu.VMEM((seqs, row_count, LANES), F32), line_rows, bands],
        (cotangent, front, rows, short_w, lines_ahead, mixed, mix, ahead, later),
        tiles,
    )

    pieces = 8
    packed = jnp.concatenate([filter_part, short_part.reshape(tiles * HALO, LANES)], axis=0)
    depth = packed.shape[0] // pieces
    piece = (depth, LANES)
    sums = pl.pallas_call(
        reduce_kernel,
        out_shape=jax.ShapeDtypeStruct((pieces, *piece), F32),
        in_specs=[pl.BlockSpec(memory_space=pltpu.VMEM)],
        out_specs=pl.BlockSpec(memory_space=pltpu.VMEM),
        scratch_shapes=[pltpu.VMEM((pieces, *piece), F32), pltpu.VMEM(piece, F32)] * 2
        + [pltpu.SemaphoreType.DMA((8,))] * 6,
        compiler_params=pltpu.CompilerParams(collective_id=1, has_side_effects=True),
    )(packed.reshape(pieces, *piece)).reshape(packed.shape)

    seq_total = seqs * lax.axis_size("dp")
    length_total = row_count * lax.axis_size("ctx")
    filter_grad = sums[:groups_here, ::-1] / math.sqrt(seq_total * length_total * (LANES // groups))
    streams = sums[groups_here:].reshape(tiles, HALO, LANES)[:, : 3 * short_w.shape[1]]
    short_sum = jnp.swapaxes(streams, 0, 1).reshape(3, short_w.shape[1], chans)
    short_grad = short_sum / math.sqrt(seq_total * length_total)
    return (block_out, jnp.swapaxes(grad, 1, 2), filter_grad, short_grad)


def solution(mesh):
    in_specs = (
        P("dp", "ctx", None, "grp"),
        P(None, None, "grp"),
        P("grp", None),
        P("ctx", "grp"),
        P("dp", "ctx", "grp"),
    )
    out_specs = (
        P("dp", "ctx", "grp"),
        P("dp", "ctx", None, "grp"),
        P("grp", None),
        P(None, None, "grp"),
    )
    return jax.shard_map(shards, mesh=mesh, in_specs=in_specs, out_specs=out_specs, check_vma=False)
```

time: 607 us -> 319 us (0.53)
  waiting for transfers between devices: 358 us -> 204 us
  local copies, waits for them, and re-layouts: 127 us -> 9.72 us
  Pallas kernels: 0 us -> 59.8 us
  other arithmetic: 56.9 us -> 3.12 us
  matrix products: 34.4 us -> 20.3 us
    psum x1 -> x0, waiting for transfers between devices: 145 us -> none  [shards(): lax.psum((filter_part, short_part), ('dp', 'ctx'))]
    reshape x14 -> x0, local copies, waits for them, and re-layouts: 65.3 us -> none  [the longest x2 31.8 us: banded(): tiled[:, :block_rows * (line_width - 1)]]
    pallas_call x0 -> x6, Pallas kernels: none -> 59.8 us  [the longest x5 36.7 us: tiled(): pl.pallas_call(kernel, grid=(tiles,), in_specs=[pl.BlockSpec(block, index...]
    convert_element_type x7 -> x1, other arithmetic: 20.8 us -> 1.75 us  [shards(): cotangent = summed.astype(BF).reshape(full)]
    unnamed x34 -> x22, local copies, waits for them, and re-layouts: 25.5 us -> 6.46 us
    dot_general x5 -> x2, matrix products: 34.4 us -> 20.3 us  [the longest x1 10.2 us: shards(): jnp.dot(flat_gated, whole_w, preferred_element_type=F32).astype(BF)]
    reduce_sum x2 -> x0, other arithmetic: 11.4 us -> none  [the longest x1 10.9 us: short_sums(): jnp.sum(feature_grad * padded[:, start:start + row_count], axis=(0, 1))]
    slice x10 -> x4, local copies, waits for them, and re-layouts: 13.2 us -> 2.46 us  [the longest x1 0.84 us: shards(): sums[groups_here:].reshape(tiles, HALO, LANES)[:, :3 * short_w.shape[1]]]
  transfers between devices with their start and end apart: 8 -> 7, of which waited for: 5 -> 4; matrix products, arithmetic and copies ran while one was open for 16% -> 4% of each run, Pallas kernels for 0% -> 7%
where the time goes in v1:
time: 319 us
  waiting for transfers between devices  204 us (64%)
  Pallas kernels  59.8 us (19%)
  matrix products  20.3 us (6%)
  between operations  13.9 us (4%)
  local copies, waits for them, and re-layouts  9.72 us (3%)
  starting transfers between devices  7.89 us (2%)
    all_gather x1, waiting for transfers between devices, shards(): whole_w = lax.all_gather(out_w, 'ctx', axis=0, tiled=True)  104 us
    reduce_scatter x1, waiting for transfers between devices, shards(): lax.psum_scatter(input_part, 'grp', scatter_dimension=1, tiled=True)  50.1 us
    all_gather x1, waiting for transfers between devices, shards(): whole_gated = lax.all_gather(gated, 'grp', axis=2, tiled=True)  38.8 us
    pallas_call x5, Pallas kernels, tiled(): pl.pallas_call(kernel, grid=(tiles,), in_specs=[pl.BlockSpec(block, index...  36.7 us
    pallas_call x1, Pallas kernels, shards(): pl.pallas_call(reduce_kernel, out_shape=jax.ShapeDtypeStruct((pieces, *pi...  23.1 us
    ppermute x4, waiting for transfers between devices, from_behind(): return lax.ppermute(block, axis, route)  10.6 us
    dot_general x1, matrix products, shards(): jnp.dot(flat_gated, whole_w, preferred_element_type=F32).astype(BF)  10.2 us
    dot_general x1, matrix products, shards(): lax.dot_general(grad_out.reshape(seqs * row_count, chans), whole_w, (((1,...  10.1 us
  transfers between devices with their start and end apart: 7, of which 4 were waited for; matrix products, arithmetic and copies ran while one was open for 4% of the time, Pallas kernels for 7%

profile of v1, /device:TPU:1, one launch (start us, length us, event | category | flops | bytes accessed | tf_op | source)
XLA Modules:
  0.0 318.6 jit_solution(12346974662809940507)
XLA Ops:
  8.0 103.6 %all-gather.5.cloned.1.call-done = bf16[4096,1024]{1,0:T(8,128)(2,1)} async-done(((bf16[128,1024]{1,0:T(8,128)(2,1)}), bf16[4096,1024]{1,0:T(8,128)(2,1)}) %all-gather.5.cloned.1.call-update) | async-done | bytes 8388624 | tf_op jit(solution)/shard_map/all_gather | solution.py:332
  111.5 10.1 %fusion.1 = f32[512,4096]{1,0:T(8,128)} fusion(bf16[512,1024]{1,0:T(8,128)(2,1)S(1)} %bitcast.17, bf16[4096,1024]{1,0:T(8,128)(2,1)} %all-gather.5.cloned.1.call-done), kind=kOutput, calls=%fused_computation.7 | convolution fusion | flops 4294967296 | bytes 17825792 | tf_op jit(solution)/shard_map/dot_general | solution.py:336
  122.4 1.9 copy-done.1
  124.3 1.3 shard_map.84
  125.6 1.8 collective-permute-start.1
  127.4 3.4 %collective-permute-start = (bf16[2,3,16,1024]{3,2,1,0:T(8,128)(2,1)S(1)}, bf16[2,3,16,1024]{3,2,1,0:T(8,128)(2,1)S(1)}, u32[]{:S(2)}, u32[]{:S(2)}) collective-permute-start(bf16[2,3,16,1024]{3,2,1,0:T(8,128)(2,1)S(1)} %slice.20), channel_id=1, source_target_pairs={{0,4},{4,8},{8,12},{12,16},{16,20},{20,24},{24,28},{28,32},{32,36}... | collective-permute-start | bytes 589832 | tf_op jit(solution)/shard_map/ppermute | solution.py:22
  131.0 10.6 %collective-permute-done.front_ref = bf16[2,3,16,1024]{3,2,1,0:T(8,128)(2,1)S(1)} collective-permute-done((bf16[2,3,16,1024]{3,2,1,0:T(8,128)(2,1)S(1)}, bf16[2,3,16,1024]{3,2,1,0:T(8,128)(2,1)S(1)}, u32[]{:S(2)}, u32[]{:S(2)}) %collective-permute-start) | collective-permute-done | bytes 196640 | tf_op jit(solution)/shard_map/ppermute | solution.py:22
  141.6 8.6 %shard_map.85 = (bf16[2,256,1024]{2,1,0:T(8,128)(2,1)}, f32[2,256,1024]{2,1,0:T(8,128)S(1)}, bf16[2,256,1024]{2,1,0:T(8,128)(2,1)S(1)}) custom-call(bf16[2,3,16,1024]{3,2,1,0:T(8,128)(2,1)S(1)} %collective-permute-done.front_ref, bf16[2,3,256,1024]{3,2,1,0:T(8,128)(2,1)} %bitcast.18, f32[3,3,1024]{2,1,0:T(4,128)S(1)} %copy-done.9, ...), custom_call_target="tpu_custom_call" | custom-call | bytes 3969024 | tf_op jit(solution)/shard_map/pallas_call | solution.py:273
  150.2 1.3 copy-done.2
  151.6 0.9 copy-done.7
  152.5 50.1 %reduce-scatter.2.cloned.1.call-done = f32[512,1024]{1,0:T(8,128)} async-done(((f32[512,4096]{1,0:T(8,128)}), f32[512,1024]{1,0:T(8,128)}) %reduce-scatter.2.cloned.1.call-update) | async-done | bytes 2097168 | tf_op jit(solution)/shard_map/reduce_scatter | solution.py:339
  202.6 1.7 convert_element_type.13
  204.4 1.6 copy-done.3
  205.9 7.2 %shard_map.86 = (bf16[2,256,1024]{2,1,0:T(8,128)(2,1)S(1)}, bf16[2,3,16,1024]{3,2,1,0:T(8,128)(2,1)}) custom-call(bf16[2,256,1024]{2,1,0:T(8,128)(2,1)S(1)} %bitcast.24, bf16[2,3,16,1024]{3,2,1,0:T(8,128)(2,1)S(1)} %collective-permute-done.front_ref, bf16[2,3,256,1024]{3,2,1,0:T(8,128)(2,1)} %bitcast.19, f32[3,3,1024]{2,1,0:T(4,128)S(1)} %copy-done.9, ...), custom_call_target="tpu_custom_call" | custom-call | bytes 6590464 | tf_op jit(solution)/shard_map/pallas_call | solution.py:273
  213.1 0.8 slice.16
  214.0 1.3 collective-permute-start.2
  215.3 1.3 collective-permute-start.3
  216.6 38.8 %all-gather.3.cloned.1.call-done = bf16[2,256,4096]{2,1,0:T(8,128)(2,1)} async-done(((bf16[2,256,1024]{2,1,0:T(8,128)(2,1)}), bf16[2,256,4096]{2,1,0:T(8,128)(2,1)}) %all-gather.3.cloned.1.call-update) | async-done | bytes 4194320 | tf_op jit(solution)/shard_map/all_gather | solution.py:333
  255.4 10.2 %convolution_convert_fusion = bf16[512,1024]{1,0:T(8,128)(2,1)} fusion(bf16[512,4096]{1,0:T(8,128)(2,1)} %bitcast.31, bf16[4096,1024]{1,0:T(8,128)(2,1)} %all-gather.5.cloned.1.call-done), kind=kOutput, calls=%fused_computation | convolution fusion | flops 4295491584 | bytes 13631488 | tf_op jit(solution)/shard_map/dot_general | solution.py:335
  265.7 5.8 %shard_map.88 = f32[64,128]{1,0:T(8,128)S(1)} custom-call(bf16[2,256,1024]{2,1,0:T(8,128)(2,1)S(1)} %get-tuple-element.13.mix_ref, bf16[2,256,1024]{2,1,0:T(8,128)(2,1)S(1)} %copy-done.8, bf16[2,128,1024]{2,1,0:T(8,128)(2,1)S(1)} %copy-done.6), custom_call_target="tpu_custom_call" | custom-call | bytes 2621440 | tf_op jit(solution)/shard_map/pallas_call | solution.py:273
  271.4 13.8 %shard_map.87 = (bf16[2,3,256,1024]{3,2,1,0:T(8,128)(2,1)}, f32[8,16,128]{2,1,0:T(8,128)S(1)}) custom-call(bf16[2,256,1024]{2,1,0:T(8,128)(2,1)S(1)} %bitcast.25, bf16[2,3,16,1024]{3,2,1,0:T(8,128)(2,1)S(1)} %collective-permute-done.front_ref, bf16[2,3,256,1024]{3,2,1,0:T(8,128)(2,1)} %bitcast.20, f32[3,3,1024]{2,1,0:T(4,128)S(1)} %copy-done.9, ...), custom_call_target="tpu_custom_call" | custom-call | bytes 8359936 | tf_op jit(solution)/shard_map/pallas_call | solution.py:273
  285.9 23.1 %shard_map.89 = f32[8,24,128]{2,1,0:T(8,128)} custom-call(f32[8,24,128]{2,1,0:T(8,128)} %bitcast.27), custom_call_target="tpu_custom_call" | custom-call | tf_op jit(solution)/shard_map/pallas_call | solution.py:373
  309.1 0.8 slice.21
  309.8 0.8 slice.22
  (36 shorter events, 3.8 us)
Async XLA Ops:
  7.2 104.4 %copy-start = (bf16[2,256,1024]{2,1,0:T(8,128)(2,1)S(1)}, bf16[2,256,1024]{2,1,0:T(8,128)(2,1)}, u32[]{:S(2)}) copy-start(bf16[2,256,1024]{2,1,0:T(8,128)(2,1)} %param.9) | copy-start | bytes 3145732
  7.2 104.3 %all-gather.5.cloned.1.call-start = ((), (), s32[]{:S(2)}) async-start(), calls=%async_computation.2 | async-start | bytes 8650752 | tf_op jit(solution)/shard_map/all_gather | solution.py:332
  7.9 194.7 %reduce-scatter.2.cloned.1.call-start = ((), (), s32[]{:S(2)}) async-start(), calls=%async_computation.3 | async-start | bytes 10485760 | tf_op jit(solution)/shard_map/reduce_scatter | solution.py:339
  121.6 0.8 copy-start.9
  121.6 9.3 %copy-start.10 = (bf16[64,128]{1,0:T(8,128)(2,1)S(1)}, bf16[64,128]{1,0:T(8,128)(2,1)}, u32[]{:S(2)}) copy-start(bf16[64,128]{1,0:T(8,128)(2,1)} %param.7) | copy-start | bytes 49156
  121.6 133.8 %all-gather.3.cloned.1.call-start = ((), (), s32[]{:S(2)}) async-start(), calls=%async_computation.1 | async-start | bytes 5242880 | tf_op jit(solution)/shard_map/all_gather | solution.py:333
  122.4 1.9 copy-start.1
  125.6 16.0 %collective-permute-start.1 = (bf16[2,128,1024]{2,1,0:T(8,128)(2,1)S(1)}, bf16[2,128,1024]{2,1,0:T(8,128)(2,1)S(1)}, u32[]{:S(2)}, u32[]{:S(2)}) collective-permute-start(bf16[2,128,1024]{2,1,0:T(8,128)(2,1)S(1)} %shard_map.84), channel_id=1, source_target_pairs={{0,4},{4,8},{8,12},{12,16},{16,20},{20,24},{24,28},{28,32},{32,36}... | collective-permute-start | bytes 1572872 | tf_op jit(solution)/shard_map/ppermute | solution.py:22
  127.4 14.2 %collective-permute-start = (bf16[2,3,16,1024]{3,2,1,0:T(8,128)(2,1)S(1)}, bf16[2,3,16,1024]{3,2,1,0:T(8,128)(2,1)S(1)}, u32[]{:S(2)}, u32[]{:S(2)}) collective-permute-start(bf16[2,3,16,1024]{3,2,1,0:T(8,128)(2,1)S(1)} %slice.20), channel_id=1, source_target_pairs={{0,4},{4,8},{8,12},{12,16},{16,20},{20,24},{24,28},{28,32},{32,36}... | collective-permute-start | bytes 589832 | tf_op jit(solution)/shard_map/ppermute | solution.py:22
  141.6 10.0 %copy-start.5 = (bf16[2,128,1024]{2,1,0:T(8,128)(2,1)}, bf16[2,128,1024]{2,1,0:T(8,128)(2,1)S(1)}, u32[]{:S(2)}) copy-start(bf16[2,128,1024]{2,1,0:T(8,128)(2,1)S(1)} %collective-permute-done.1.behind_ref) | copy-start | bytes 1572868
  150.2 1.3 copy-start.2
  151.6 1.0 copy-start.7
  204.4 1.6 copy-start.3
  214.0 57.5 %collective-permute-start.2 = (bf16[2,128,1024]{2,1,0:T(8,128)(2,1)}, bf16[2,128,1024]{2,1,0:T(8,128)(2,1)}, u32[]{:S(2)}, u32[]{:S(2)}) collective-permute-start(bf16[2,128,1024]{2,1,0:T(8,128)(2,1)} %slice.16), channel_id=1, source_target_pairs={{4,0},{8,4},{12,8},{16,12},{20,16},{24,20},{28,24},{32,28},{36,32}... | collective-permute-start | bytes 1572872 | tf_op jit(solution)/shard_map/ppermute | solution.py:22
  215.3 56.2 %collective-permute-start.3 = (bf16[2,3,16,1024]{3,2,1,0:T(8,128)(2,1)}, bf16[2,3,16,1024]{3,2,1,0:T(8,128)(2,1)}, u32[]{:S(2)}, u32[]{:S(2)}) collective-permute-start(bf16[2,3,16,1024]{3,2,1,0:T(8,128)(2,1)} %get-tuple-element.14), channel_id=1, source_target_pairs={{4,0},{8,4},{12,8},{16,12},{20,16},{24,20},{28,24},{32,28},{36,32}... | collective-permute-start | bytes 589832 | tf_op jit(solution)/shard_map/ppermute | solution.py:22
  255.4 10.3 %copy-start.6 = (bf16[2,128,1024]{2,1,0:T(8,128)(2,1)S(1)}, bf16[2,128,1024]{2,1,0:T(8,128)(2,1)}, u32[]{:S(2)}) copy-start(bf16[2,128,1024]{2,1,0:T(8,128)(2,1)} %copy-done.5) | copy-start | bytes 1572868
  255.4 10.3 %copy-start.8 = (bf16[2,256,1024]{2,1,0:T(8,128)(2,1)S(1)}, bf16[2,256,1024]{2,1,0:T(8,128)(2,1)}, u32[]{:S(2)}) copy-start(bf16[2,256,1024]{2,1,0:T(8,128)(2,1)} %copy-done.7) | copy-start | bytes 3145732
  255.4 16.0 %copy-start.4 = (f32[2,256,1024]{2,1,0:T(8,128)S(1)}, f32[2,256,1024]{2,1,0:T(8,128)}, u32[]{:S(2)}) copy-start(f32[2,256,1024]{2,1,0:T(8,128)} %copy-done.2) | copy-start | bytes 6291460
Sparse Core Ops, SparseCore 0:
  10.6 100.9 all-gather.4
  121.8 80.7 reduce-scatter.1
  205.0 50.3 all-gather.2

commit v2 on v1

--- a/solution.py
+++ b/solution.py
@@ -14,6 +14,7 @@
 BLOCK = 128
 HALO = 16
 MESH = pl.DeviceIdType.MESH
+ALONG_Z = 8
 
 
 def from_behind(block, axis, distance):
@@ -268,6 +269,220 @@
         second(step).wait_send()
 
 
+def exchange_kernel(
+    along_z, w_ref, gated_ref, cotangent_ref, out_ref, grad_ref,
+    whole, gathered, to_a, to_b, from_a, from_b, to_right, to_left, from_left, from_right,
+    kept_right, kept_left, own,
+    z_send, z_recv, up_send, up_recv, down_send, down_recv, far_send, far_recv,
+    pair_send, pair_recv, x_send, x_recv, sum_send, sum_recv,
+):
+    ctx, core, x = lax.axis_index("ctx"), lax.axis_index("dp"), lax.axis_index("grp")
+    lines, ring = lax.axis_size("ctx") // along_z, lax.axis_size("grp")
+    y, z = ctx // along_z, ctx % along_z
+    part = w_ref.shape[0] // 2
+    total, chans = gated_ref.shape
+    half = total // 2
+
+    def at_z(step):
+        return {"ctx": y * along_z + (z + along_z + step) % along_z}
+
+    def at_y(step):
+        return {"ctx": (y + lines + step) % lines * along_z + z}
+
+    def at_x(step):
+        return {"grp": (x + ring + step) % ring}
+
+    partner = {"dp": 1 - core}
+    barrier = pltpu.get_barrier_semaphore()
+    for device in (at_z(1), at_z(-1), at_y(1), at_y(-1), at_x(1), at_x(-1), partner):
+        pl.semaphore_signal(barrier, inc=1, device_id=device, device_id_type=MESH)
+    pl.semaphore_wait(barrier, 7)
+
+    def copy(src, dst, send, recv, device):
+        return pltpu.make_async_remote_copy(
+            src_ref=src, dst_ref=dst, send_sem=send, recv_sem=recv, device_id=device, device_id_type=MESH
+        )
+
+    def block(step_y, step_z, carrier):
+        row = ((y + lines + step_y) % lines * along_z + (z + along_z + step_z) % along_z) * 2 + carrier
+        return whole.at[pl.ds(pl.multiple_of(row * part, part), part), :]
+
+    steps = [0]
+    for k in range(1, along_z // 2 + 1):
+        steps += [-k, k] if 2 * k < along_z else [-k]
+    started = []
+
+    def go(*what):
+        started.append(copy(*what))
+        started[-1].start()
+
+    def hand_over(kind, step_y, u):
+        place = kind * along_z + u
+        mine = block(step_y, steps[u], core)
+        go(mine, mine, pair_send.at[place], pair_recv.at[place], partner)
+
+    def y_turn(u):
+        behind, ahead = block(-1, steps[u], core), block(1, steps[u], core)
+        copy(behind, behind, up_send.at[u], up_recv.at[u], at_y(1)).wait_recv()
+        if u % 2 == 0:
+            go(behind, behind, far_send.at[u], far_recv.at[u], at_y(1))
+        hand_over(1, -1, u)
+        copy(ahead, ahead, down_send.at[u], down_recv.at[u], at_y(-1)).wait_recv()
+        if u % 2 == 1:
+            go(ahead, ahead, far_send.at[u], far_recv.at[u], at_y(-1))
+        hand_over(2, 1, u)
+
+    def far_turn(u):
+        far = block(2, steps[u], core)
+        copy(far, far, far_send.at[u], far_recv.at[u], at_y(1)).wait_recv()
+        hand_over(3, 2, u)
+
+    chunks = 4
+    tall = total // chunks
+
+    def rows_of(c):
+        return pl.ds(c * tall, tall)
+
+    def x_start(c):
+        src = gated_ref.at[rows_of(c), :]
+        go(src, gathered.at[0, rows_of(c), :], x_send.at[0, c], x_recv.at[0, c], at_x(1))
+        go(src, gathered.at[1, rows_of(c), :], x_send.at[1, c], x_recv.at[1, c], at_x(-1))
+
+    def x_wait(slot, c):
+        here = gathered.at[slot, rows_of(c), :]
+        copy(here, here, x_send.at[slot, c], x_recv.at[slot, c], at_x(1)).wait_recv()
+
+    def x_turn(c):
+        x_wait(0, c)
+        x_wait(1, c)
+        slot, to = (0, at_x(1)) if c < chunks // 2 else (1, at_x(-1))
+        go(gathered.at[slot, rows_of(c), :], gathered.at[2, rows_of(c), :], x_send.at[2, c], x_recv.at[2, c], to)
+
+    own_part = w_ref.at[pl.ds(pl.multiple_of(core * part, part), part), :]
+    x_next = 0
+    for c in range(chunks):
+        x_start(c)
+    for u in range(along_z):
+        mine = own_part
+        if u > 0:
+            mine = block(0, steps[u], core)
+            copy(mine, mine, z_send.at[u], z_recv.at[u], at_z(1)).wait_recv()
+        for direction in (-1, 1):
+            onward = steps[u] + direction
+            if onward in steps and (u == 0 or steps[u] * direction > 0):
+                v = steps.index(onward)
+                go(mine, block(0, steps[u], core), z_send.at[v], z_recv.at[v], at_z(-direction))
+        go(mine, block(0, steps[u], core), up_send.at[u], up_recv.at[u], at_y(1))
+        go(mine, block(0, steps[u], core), down_send.at[u], down_recv.at[u], at_y(-1))
+        if u > 0:
+            hand_over(0, 0, u)
+            y_turn(u - 1)
+        if u > 1:
+            far_turn(u - 2)
+        if u % 2 == 1 and x_next < chunks:
+            x_turn(x_next)
+            x_next += 1
+    whole[pl.ds(pl.multiple_of(ctx * 2 * part, 2 * part), 2 * part), :] = w_ref[...]
+    y_turn(along_z - 1)
+    for c in range(x_next, chunks):
+        x_turn(c)
+    for u in range(max(along_z - 2, 0), along_z):
+        far_turn(u)
+    for kind, step_y in enumerate((0, -1, 1, 2)):
+        for u in range(along_z):
+            if kind == 0 and u == 0:
+                continue
+            place = kind * along_z + u
+            other = block(step_y, steps[u], 1 - core)
+            copy(other, other, pair_send.at[place], pair_recv.at[place], partner).wait_recv()
+
+    wide = min(chans, 256)
+    right, left, across = (x + 1) % ring, (x + ring - 1) % ring, (x + 2) % ring
+
+    def columns(j):
+        return pl.ds(pl.multiple_of(j * wide, wide), wide)
+
+    def partial(owner, j):
+        rows = whole[pl.ds(pl.multiple_of(owner * chans + j * wide, wide), wide), :]
+        return lax.dot_general(cotangent_ref[...], rows, (((1,), (1,)), ((), ())), preferred_element_type=F32)
+
+    def far_sums(j, carry):
+        found = partial(across, j)
+        to_a[:, columns(j)] = found[:half].astype(BF)
+        to_b[:, columns(j)] = found[half:].astype(BF)
+        return carry
+
+    def near_sums(j, carry):
+        found = partial(right, j)
+        kept_right[:, columns(j)] = found[:half]
+        to_right[half:, columns(j)] = found[half:].astype(BF)
+        found = partial(left, j)
+        to_left[:half, columns(j)] = found[:half].astype(BF)
+        kept_left[:, columns(j)] = found[half:]
+        return carry
+
+    def outputs(j, carry):
+        own[:, columns(j)] = partial(x, j)
+        found = None
+        for slot, owner in ((None, x), (0, left), (1, right), (2, across)):
+            rows = whole[pl.ds(pl.multiple_of(owner * chans, chans), chans), columns(j)]
+            source = gated_ref[...] if slot is None else gathered[slot]
+            term = jnp.dot(source, rows, preferred_element_type=F32)
+            found = term if found is None else found + term
+        out_ref[:, columns(j)] = found.astype(BF)
+        return carry
+
+    first, second = pl.ds(0, half), pl.ds(half, half)
+    lax.fori_loop(0, chans // wide, far_sums, 0)
+    go(to_a, from_a, sum_send.at[0], sum_recv.at[0], at_x(1))
+    go(to_b, from_b, sum_send.at[1], sum_recv.at[1], at_x(-1))
+    lax.fori_loop(0, chans // wide, near_sums, 0)
+    go(to_right.at[second, :], from_left.at[second, :], sum_send.at[2], sum_recv.at[2], at_x(1))
+    go(to_left.at[first, :], from_right.at[first, :], sum_send.at[3], sum_recv.at[3], at_x(-1))
+    for c in range(chunks):
+        x_wait(2, c)
+    lax.fori_loop(0, chans // wide, outputs, 0)
+    copy(to_a, from_a, sum_send.at[0], sum_recv.at[0], at_x(1)).wait_recv()
+    to_right[:half, :] = (kept_right[...] + from_a[...].astype(F32)).astype(BF)
+    go(to_right.at[first, :], from_left.at[first, :], sum_send.at[4], sum_recv.at[4], at_x(1))
+    copy(to_b, from_b, sum_send.at[1], sum_recv.at[1], at_x(-1)).wait_recv()
+    to_left[half:, :] = (kept_left[...] + from_b[...].astype(F32)).astype(BF)
+    go(to_left.at[second, :], from_right.at[second, :], sum_send.at[5], sum_recv.at[5], at_x(-1))
+    for ref, rows, n in ((from_left, second, 2), (from_right, first, 3), (from_left, first, 4), (from_right, second, 5)):
+        here = ref.at[rows, :]
+        copy(here, here, sum_send.at[n], sum_recv.at[n], at_x(1)).wait_recv()
+    grad_ref[...] = (own[...] + (from_left[...].astype(F32) + from_right[...].astype(F32))).astype(BF)
+    for sent in started:
+        sent.wait_send()
+
+
+def exchange(out_w, gated, grad_out):
+    total, chans = gated.shape
+    depth = out_w.shape[0] * lax.axis_size("ctx")
+    half = (total // 2, chans)
+    dma = pltpu.SemaphoreType.DMA
+    flops = 4 * total * depth * chans
+    return pl.pallas_call(
+        functools.partial(exchange_kernel, ALONG_Z),
+        out_shape=[jax.ShapeDtypeStruct(gated.shape, BF)] * 2,
+        in_specs=[pl.BlockSpec(memory_space=pltpu.VMEM)] * 3,
+        out_specs=[pl.BlockSpec(memory_space=pltpu.VMEM)] * 2,
+        scratch_shapes=[pltpu.VMEM((depth, chans), BF), pltpu.VMEM((3, total, chans), BF)]
+        + [pltpu.VMEM(half, BF)] * 4
+        + [pltpu.VMEM(gated.shape, BF)] * 4
+        + [pltpu.VMEM(half, F32)] * 2
+        + [pltpu.VMEM(gated.shape, F32)]
+        + [dma((ALONG_Z,))] * 8
+        + [dma((4 * ALONG_Z,))] * 2
+        + [dma((3, 4))] * 2
+        + [dma((6,))] * 2,
+        cost_estimate=pl.CostEstimate(flops=flops, bytes_accessed=8 * total * chans, transcendentals=0),
+        compiler_params=pltpu.CompilerParams(
+            collective_id=2, has_side_effects=True, vmem_limit_bytes=52 << 20
+        ),
+    )(out_w, gated, grad_out)
+
+
 def tiled(kernel, ins, outs, scratch, arrays, tiles, flops=0):
     read = sum(math.prod(a.shape) * a.dtype.itemsize for a in arrays)
     return pl.pallas_call(
@@ -329,15 +544,9 @@
         tiles,
     )
 
-    whole_w = lax.all_gather(out_w, "ctx", axis=0, tiled=True)
-    whole_gated = lax.all_gather(gated, "grp", axis=2, tiled=True)
-    flat_gated = whole_gated.reshape(seqs * row_count, whole_gated.shape[2])
-    block_out = jnp.dot(flat_gated, whole_w, preferred_element_type=F32).astype(BF).reshape(full)
-    input_part = lax.dot_general(
-        grad_out.reshape(seqs * row_count, chans), whole_w, (((1,), (1,)), ((), ())), preferred_element_type=F32
-    )
-    summed = lax.psum_scatter(input_part, "grp", scatter_dimension=1, tiled=True)
-    cotangent = summed.astype(BF).reshape(full)
+    flat = (seqs * row_count, chans)
+    block_out, cotangent = exchange(out_w, gated.reshape(flat), grad_out.reshape(flat))
+    block_out, cotangent = block_out.reshape(full), cotangent.reshape(full)
 
     mix, head = tiled(
         mix_kernel,
@@ -366,16 +575,20 @@
         tiles,
     )
 
-    pieces = 8
+    pieces = ALONG_Z
     packed = jnp.concatenate([filter_part, short_part.reshape(tiles * HALO, LANES)], axis=0)
     depth = packed.shape[0] // pieces
     piece = (depth, LANES)
+    peers = 2 * (lax.axis_size("ctx") // pieces)
     sums = pl.pallas_call(
         reduce_kernel,
         out_shape=jax.ShapeDtypeStruct((pieces, *piece), F32),
         in_specs=[pl.BlockSpec(memory_space=pltpu.VMEM)],
         out_specs=pl.BlockSpec(memory_space=pltpu.VMEM),
-        scratch_shapes=[pltpu.VMEM((pieces, *piece), F32), pltpu.VMEM(piece, F32)] * 2
+        scratch_shapes=[
+            pltpu.VMEM((pieces, *piece), F32), pltpu.VMEM(piece, F32),
+            pltpu.VMEM((peers, *piece), F32), pltpu.VMEM(piece, F32),
+        ]
         + [pltpu.SemaphoreType.DMA((8,))] * 6,
         compiler_params=pltpu.CompilerParams(collective_id=1, has_side_effects=True),
     )(packed.reshape(pieces, *piece)).reshape(packed.shape)

time: 319 us -> 193 us (0.61)
  waiting for transfers between devices: 204 us -> 22.2 us
  Pallas kernels: 59.8 us -> 149 us
  matrix products: 20.3 us -> 0 us
  between operations: 13.9 us -> 0.78 us
    all_gather x2 -> x0, waiting for transfers between devices: 142 us -> none  [the longest x1 104 us: shards(): whole_w = lax.all_gather(out_w, 'ctx', axis=0, tiled=True)]
    pallas_call x0 -> x1, Pallas kernels: none -> 91.2 us  [exchange(): pl.pallas_call(functools.partial(exchange_kernel, ALONG_Z), out_shape=[ja...]
    reduce_scatter x1 -> x0, waiting for transfers between devices: 50.1 us -> none  [shards(): lax.psum_scatter(input_part, 'grp', scatter_dimension=1, tiled=True)]
    dot_general x2 -> x0, matrix products: 20.3 us -> none  [the longest x1 10.2 us: shards(): jnp.dot(flat_gated, whole_w, preferred_element_type=F32).astype(BF)]
    ppermute x4, waiting for transfers between devices: 10.6 us -> 22.2 us  [from_behind(): return lax.ppermute(block, axis, route)]
    unnamed x22 -> x15, local copies, waits for them, and re-layouts: 6.46 us -> 5.85 us
  transfers between devices with their start and end apart: 7 -> 4, of which waited for: 4 -> 2; matrix products, arithmetic and copies ran while one was open for 4% -> 0% of each run, Pallas kernels for 7% -> 3%
where the time goes in v2:
time: 193 us; the launch traced here: 192 us
  Pallas kernels  149 us (77%)
  waiting for transfers between devices  22.2 us (12%)
  starting transfers between devices  10.6 us (5%)
  local copies, waits for them, and re-layouts  8.3 us (4%)
    pallas_call x1, Pallas kernels, exchange(): pl.pallas_call(functools.partial(exchange_kernel, ALONG_Z), out_shape=[ja...  91.2 us
    pallas_call x5, Pallas kernels, tiled(): pl.pallas_call(kernel, grid=(tiles,), in_specs=[pl.BlockSpec(block, index...  35.5 us
    ppermute x4, waiting for transfers between devices, from_behind(): return lax.ppermute(block, axis, route)  22.2 us
    pallas_call x1, Pallas kernels, shards(): pl.pallas_call(reduce_kernel, out_shape=jax.ShapeDtypeStruct((pieces, *pi...  22.1 us
    ppermute x4, starting transfers between devices, from_behind(): return lax.ppermute(block, axis, route)  10.6 us
    unnamed x15, local copies, waits for them, and re-layouts  5.85 us
  transfers between devices with their start and end apart: 4, of which 2 were waited for; matrix products, arithmetic and copies ran while one was open for 0% of the time, Pallas kernels for 3%

profile of v2, /device:TPU:1, one launch (start us, length us, event | category | flops | bytes accessed | tf_op | source)
XLA Modules:
  0.0 192.1 jit_solution(5466175111196920649)
XLA Ops:
  0.6 1.9 copy-done
  2.5 0.8 copy-done.2
  3.3 1.3 shard_map.84
  4.7 4.5 %collective-permute-start.1 = (bf16[2,128,1024]{2,1,0:T(8,128)(2,1)S(1)}, bf16[2,128,1024]{2,1,0:T(8,128)(2,1)S(1)}, u32[]{:S(2)}, u32[]{:S(2)}) collective-permute-start(bf16[2,128,1024]{2,1,0:T(8,128)(2,1)S(1)} %shard_map.84), channel_id=1, source_target_pairs={{0,4},{4,8},{8,12},{12,16},{16,20},{20,24},{24,28},{28,32},{32,36}... | collective-permute-start | bytes 1572872 | tf_op jit(solution)/shard_map/ppermute | solution.py:23
  9.2 3.5 %collective-permute-start = (bf16[2,3,16,1024]{3,2,1,0:T(8,128)(2,1)S(1)}, bf16[2,3,16,1024]{3,2,1,0:T(8,128)(2,1)S(1)}, u32[]{:S(2)}, u32[]{:S(2)}) collective-permute-start(bf16[2,3,16,1024]{3,2,1,0:T(8,128)(2,1)S(1)} %slice.20), channel_id=1, source_target_pairs={{0,4},{4,8},{8,12},{12,16},{16,20},{20,24},{24,28},{28,32},{32,36}... | collective-permute-start | bytes 589832 | tf_op jit(solution)/shard_map/ppermute | solution.py:23
  12.8 0.1 rev.6
  12.9 11.0 %collective-permute-done.front_ref = bf16[2,3,16,1024]{3,2,1,0:T(8,128)(2,1)S(1)} collective-permute-done((bf16[2,3,16,1024]{3,2,1,0:T(8,128)(2,1)S(1)}, bf16[2,3,16,1024]{3,2,1,0:T(8,128)(2,1)S(1)}, u32[]{:S(2)}, u32[]{:S(2)}) %collective-permute-start) | collective-permute-done | bytes 196640 | tf_op jit(solution)/shard_map/ppermute | solution.py:23
  24.0 8.0 %shard_map.85 = (bf16[2,256,1024]{2,1,0:T(8,128)(2,1)S(1)}, f32[2,256,1024]{2,1,0:T(8,128)S(1)}, bf16[2,256,1024]{2,1,0:T(8,128)(2,1)S(1)}) custom-call(bf16[2,3,16,1024]{3,2,1,0:T(8,128)(2,1)S(1)} %collective-permute-done.front_ref, bf16[2,3,256,1024]{3,2,1,0:T(8,128)(2,1)} %bitcast.13, f32[3,3,1024]{2,1,0:T(4,128)S(1)} %copy-done.3, ...), custom_call_target="tpu_custom_call" | custom-call | bytes 3969024 | tf_op jit(solution)/shard_map/pallas_call | solution.py:488
  32.0 1.0 copy-done.4
  32.9 91.2 %shard_map.86 = (bf16[512,1024]{1,0:T(8,128)(2,1)S(1)}, bf16[512,1024]{1,0:T(8,128)(2,1)}) custom-call(bf16[128,1024]{1,0:T(8,128)(2,1)S(1)} %copy-done.5, bf16[512,1024]{1,0:T(8,128)(2,1)} %bitcast.23, bf16[512,1024]{1,0:T(8,128)(2,1)} %bitcast.29), custom_call_target="tpu_custom_call" | custom-call | flops 8589934592 | bytes 4194304 | tf_op jit(solution)/shard_map/pallas_call | solution.py:465
  124.2 1.2 copy-done.1
  125.4 6.5 %shard_map.87 = (bf16[2,256,1024]{2,1,0:T(8,128)(2,1)S(1)}, bf16[2,3,16,1024]{3,2,1,0:T(8,128)(2,1)S(1)}) custom-call(bf16[2,256,1024]{2,1,0:T(8,128)(2,1)S(1)} %bitcast.19, bf16[2,3,16,1024]{3,2,1,0:T(8,128)(2,1)S(1)} %collective-permute-done.front_ref, bf16[2,3,256,1024]{3,2,1,0:T(8,128)(2,1)} %bitcast.14, f32[3,3,1024]{2,1,0:T(4,128)S(1)} %copy-done.3, ...), custom_call_target="tpu_custom_call" | custom-call | bytes 6590464 | tf_op jit(solution)/shard_map/pallas_call | solution.py:488
  132.0 1.3 collective-permute-start.2
  133.3 1.3 collective-permute-start.3
  134.6 5.8 %shard_map.89 = f32[64,128]{1,0:T(8,128)S(1)} custom-call(bf16[2,256,1024]{2,1,0:T(8,128)(2,1)S(1)} %get-tuple-element.17.mix_ref, bf16[2,256,1024]{2,1,0:T(8,128)(2,1)S(1)} %get-tuple-element.20.product_ref, bf16[2,128,1024]{2,1,0:T(8,128)(2,1)S(1)} %collective-permute-done.1.behind_ref), custom_call_target="tpu_custom_call" | custom-call | bytes 2621440 | tf_op jit(solution)/shard_map/pallas_call | solution.py:488
  140.3 11.2 %collective-permute-done.3.next_ref = bf16[2,3,16,1024]{3,2,1,0:T(8,128)(2,1)S(1)} collective-permute-done((bf16[2,3,16,1024]{3,2,1,0:T(8,128)(2,1)S(1)}, bf16[2,3,16,1024]{3,2,1,0:T(8,128)(2,1)S(1)}, u32[]{:S(2)}, u32[]{:S(2)}) %collective-permute-start.3) | collective-permute-done | bytes 196640 | tf_op jit(solution)/shard_map/ppermute | solution.py:23
  151.5 13.9 %shard_map.88 = (bf16[2,3,256,1024]{3,2,1,0:T(8,128)(2,1)}, f32[8,16,128]{2,1,0:T(8,128)S(1)}) custom-call(bf16[2,256,1024]{2,1,0:T(8,128)(2,1)S(1)} %bitcast.20, bf16[2,3,16,1024]{3,2,1,0:T(8,128)(2,1)S(1)} %collective-permute-done.front_ref, bf16[2,3,256,1024]{3,2,1,0:T(8,128)(2,1)} %bitcast.15, f32[3,3,1024]{2,1,0:T(4,128)S(1)} %copy-done.3, ...), custom_call_target="tpu_custom_call" | custom-call | bytes 8359936 | tf_op jit(solution)/shard_map/pallas_call | solution.py:488
  165.4 0.6 pad_maximum_fusion
  166.1 22.1 %shard_map.90 = f32[8,24,128]{2,1,0:T(8,128)} custom-call(f32[8,24,128]{2,1,0:T(8,128)} %bitcast.24), custom_call_target="tpu_custom_call" | custom-call | tf_op jit(solution)/shard_map/pallas_call | solution.py:583
  188.2 0.8 slice.21
  188.9 0.8 slice.22
  189.9 0.6 broadcast_multiply_fusion
  190.5 0.6 div.21
  191.2 1.0 copy.15
  (18 shorter events, 0.3 us)
Async XLA Ops:
  0.6 1.9 copy-start
  2.5 0.8 copy-start.2
  3.3 9.4 %copy-start.6 = (bf16[64,128]{1,0:T(8,128)(2,1)S(1)}, bf16[64,128]{1,0:T(8,128)(2,1)}, u32[]{:S(2)}) copy-start(bf16[64,128]{1,0:T(8,128)(2,1)} %param.7) | copy-start | bytes 49156
  3.3 20.7 %copy-start.3 = (f32[3,3,1024]{2,1,0:T(4,128)S(1)}, f32[3,3,1024]{2,1,0:T(4,128)}, u32[]{:S(2)}) copy-start(f32[3,3,1024]{2,1,0:T(4,128)} %taps_ref.7) | copy-start | bytes 110596
  4.7 28.3 %copy-start.5 = (bf16[128,1024]{1,0:T(8,128)(2,1)S(1)}, bf16[128,1024]{1,0:T(8,128)(2,1)}, u32[]{:S(2)}) copy-start(bf16[128,1024]{1,0:T(8,128)(2,1)} %w_ref.1) | copy-start | bytes 786436
  4.7 19.3 %collective-permute-start.1 = (bf16[2,128,1024]{2,1,0:T(8,128)(2,1)S(1)}, bf16[2,128,1024]{2,1,0:T(8,128)(2,1)S(1)}, u32[]{:S(2)}, u32[]{:S(2)}) collective-permute-start(bf16[2,128,1024]{2,1,0:T(8,128)(2,1)S(1)} %shard_map.84), channel_id=1, source_target_pairs={{0,4},{4,8},{8,12},{12,16},{16,20},{20,24},{24,28},{28,32},{32,36}... | collective-permute-start | bytes 1572872 | tf_op jit(solution)/shard_map/ppermute | solution.py:23
  9.2 14.7 %collective-permute-start = (bf16[2,3,16,1024]{3,2,1,0:T(8,128)(2,1)S(1)}, bf16[2,3,16,1024]{3,2,1,0:T(8,128)(2,1)S(1)}, u32[]{:S(2)}, u32[]{:S(2)}) collective-permute-start(bf16[2,3,16,1024]{3,2,1,0:T(8,128)(2,1)S(1)} %slice.20), channel_id=1, source_target_pairs={{0,4},{4,8},{8,12},{12,16},{16,20},{20,24},{24,28},{28,32},{32,36}... | collective-permute-start | bytes 589832 | tf_op jit(solution)/shard_map/ppermute | solution.py:23
  32.0 1.0 copy-start.4
  124.1 1.2 copy-start.1
  132.0 19.5 %collective-permute-start.2 = (bf16[2,128,1024]{2,1,0:T(8,128)(2,1)S(1)}, bf16[2,128,1024]{2,1,0:T(8,128)(2,1)S(1)}, u32[]{:S(2)}, u32[]{:S(2)}) collective-permute-start(bf16[2,128,1024]{2,1,0:T(8,128)(2,1)S(1)} %slice.16), channel_id=1, source_target_pairs={{4,0},{8,4},{12,8},{16,12},{20,16},{24,20},{28,24},{32,28},{36,32}... | collective-permute-start | bytes 1572872 | tf_op jit(solution)/shard_map/ppermute | solution.py:23
  133.3 18.2 %collective-permute-start.3 = (bf16[2,3,16,1024]{3,2,1,0:T(8,128)(2,1)S(1)}, bf16[2,3,16,1024]{3,2,1,0:T(8,128)(2,1)S(1)}, u32[]{:S(2)}, u32[]{:S(2)}) collective-permute-start(bf16[2,3,16,1024]{3,2,1,0:T(8,128)(2,1)S(1)} %get-tuple-element.18), channel_id=1, source_target_pairs={{4,0},{8,4},{12,8},{16,12},{20,16},{24,20},{28,24},{32,28},{36,32}... | collective-permute-start | bytes 589832 | tf_op jit(solution)/shard_map/ppermute | solution.py:23

commit v3 on v1

--- a/solution.py
+++ b/solution.py
@@ -14,12 +14,7 @@
 BLOCK = 128
 HALO = 16
 MESH = pl.DeviceIdType.MESH
-
-
-def from_behind(block, axis, distance):
-    devices = range(lax.axis_size(axis))
-    route = [(i - distance, i) for i in devices if i - distance in devices]
-    return lax.ppermute(block, axis, route)
+ALONG_Z = 8
 
 
 def fill(scratch, front, rows):
@@ -36,12 +31,12 @@
     return total
 
 
-def band_rows(lines, band):
+def band_rows(lines, band, count=BLOCK):
     groups = lines.shape[0]
     for g in range(groups):
-        line = jnp.broadcast_to(lines[g : g + 1, :], (BLOCK, lines.shape[1]))
+        line = jnp.broadcast_to(lines[g : g + 1, :], (count, lines.shape[1]))
         turned = pltpu.roll(line, 0, 1, stride=1, stride_axis=0)
-        band[g * BLOCK : (g + 1) * BLOCK, :] = turned.astype(BF)
+        band[g * count : (g + 1) * count, :] = turned.astype(BF)
 
 
 def group_of_lane(shape, groups):
@@ -49,17 +44,17 @@
     return (lane % LANES) // (LANES // groups)
 
 
-def own_group(wide, groups):
-    owner = group_of_lane((BLOCK, wide.shape[1]), groups)
-    kept = wide[0:BLOCK]
+def own_group(wide, groups, count=BLOCK):
+    owner = group_of_lane((count, wide.shape[1]), groups)
+    kept = wide[0:count]
     for g in range(1, groups):
-        kept = jnp.where(owner == g, wide[g * BLOCK : (g + 1) * BLOCK], kept)
+        kept = jnp.where(owner == g, wide[g * count : (g + 1) * count], kept)
     return kept
 
 
-def window_pair(padded, start):
+def window_pair(padded, start, lanes=slice(None)):
     return jnp.concatenate(
-        [padded[s, start : start + 2 * BLOCK, :] for s in range(padded.shape[0])], axis=1
+        [padded[s, start : start + 2 * BLOCK, lanes] for s in range(padded.shape[0])], axis=1
     )
 
 
@@ -72,66 +67,10 @@
         out_ref[s] = (found[0] * found[1]).astype(BF)
 
 
-def forward_kernel(
-    front_ref, rows_ref, taps_ref, lines_ref, behind_ref,
-    gated_ref, mixed_ref, product_ref, scratch, padded, queries, band,
-):
-    seqs, row_count = rows_ref.shape[0], rows_ref.shape[2]
-    groups = lines_ref.shape[0]
-    band_rows(lines_ref[...], band)
-    for s in range(seqs):
-        found = []
-        for stream in range(3):
-            fill(scratch, front_ref[s, stream], rows_ref[s, stream])
-            found.append(feature(scratch, taps_ref, stream, row_count))
-        queries[s] = found[0]
-        product = (found[1] * found[2]).astype(BF)
-        product_ref[s] = product
-        padded[s, 0:BLOCK, :] = behind_ref[s]
-        padded[s, BLOCK : BLOCK + row_count, :] = product
-    for b in range(row_count // BLOCK):
-        here = slice(b * BLOCK, (b + 1) * BLOCK)
-        wide = jnp.dot(
-            band[...], window_pair(padded, b * BLOCK), preferred_element_type=F32
-        )
-        kept = own_group(wide, groups)
-        for s in range(seqs):
-            mixed = kept[:, s * LANES : (s + 1) * LANES]
-            mixed_ref[s, here, :] = mixed
-            gated_ref[s, here, :] = (queries[s, here, :] * mixed).astype(BF)
-
-
-def mix_kernel(
-    cotangent_ref, front_ref, rows_ref, taps_ref, lines_ref, mixed_ref,
-    mix_ref, head_ref, scratch, band,
-):
-    seqs, row_count = rows_ref.shape[0], rows_ref.shape[2]
-    groups = lines_ref.shape[0]
-    band_rows(lines_ref[...], band)
-    for s in range(seqs):
-        fill(scratch, front_ref[s, 0], rows_ref[s, 0])
-        query = feature(scratch, taps_ref, 0, row_count)
-        mix_ref[s] = (cotangent_ref[s].astype(F32) * query).astype(BF)
-    wide = jnp.dot(band[...], window_pair(mix_ref, 0), preferred_element_type=F32)
-    kept = own_group(wide, groups)
-    for s in range(seqs):
-        pulled = kept[0:HALO, s * LANES : (s + 1) * LANES]
-        found = []
-        for stream in (1, 2):
-            fill(scratch, front_ref[s, stream], rows_ref[s, stream, 0:HALO])
-            found.append(feature(scratch, taps_ref, stream, HALO))
-        head_ref[s, 0] = (cotangent_ref[s, 0:HALO, :].astype(F32) * mixed_ref[s, 0:HALO, :]).astype(BF)
-        head_ref[s, 1] = (pulled * found[1]).astype(BF)
-        head_ref[s, 2] = (pulled * found[0]).astype(BF)
-
-
-def filter_kernel(mix_ref, product_ref, behind_ref, sums_ref, padded):
-    seqs, row_count = product_ref.shape[0], product_ref.shape[1]
+def filter_kernel(mix_ref, padded_ref, sums_ref):
+    seqs, row_count = padded_ref.shape[0], padded_ref.shape[1] - BLOCK
     groups = sums_ref.shape[0]
     blocks = row_count // BLOCK
-    for s in range(seqs):
-        padded[s, 0:BLOCK, :] = behind_ref[s]
-        padded[s, BLOCK : BLOCK + row_count, :] = product_ref[s]
     rows = lax.broadcasted_iota(jnp.int32, (BLOCK, BLOCK), 0)
     columns = lax.broadcasted_iota(jnp.int32, (BLOCK, BLOCK), 1)
     upturn = (rows + columns == BLOCK - 1).astype(BF)
@@ -139,7 +78,7 @@
     for s in range(seqs):
         for b in range(blocks):
             parts.append(mix_ref[s, b * BLOCK : (b + 1) * BLOCK, :])
-            wins.append(padded[s, b * BLOCK : (b + 2) * BLOCK, :])
+            wins.append(padded_ref[s, b * BLOCK : (b + 2) * BLOCK, :])
     grads = jnp.dot(upturn, jnp.concatenate(parts, axis=1), preferred_element_type=F32)
     windows = jnp.concatenate(wins, axis=1)
     owner = group_of_lane(grads.shape, groups)
@@ -156,18 +95,15 @@
 
 def backward_kernel(
     cotangent_ref, front_ref, rows_ref, taps_ref, lines_ref, mixed_ref,
-    mix_ref, ahead_ref, next_ref, grad_ref, short_ref, scratch, padded, pulled, later, band,
+    padded_ref, next_ref, grad_ref, short_ref, scratch, pulled, later, band,
 ):
     seqs, row_count = rows_ref.shape[0], rows_ref.shape[2]
     groups = lines_ref.shape[0]
     taps = taps_ref.shape[1]
     band_rows(lines_ref[...], band)
-    for s in range(seqs):
-        padded[s, 0:row_count, :] = mix_ref[s]
-        padded[s, row_count : row_count + BLOCK, :] = ahead_ref[s]
     for b in range(row_count // BLOCK):
         wide = jnp.dot(
-            band[...], window_pair(padded, b * BLOCK), preferred_element_type=F32
+            band[...], window_pair(padded_ref, b * BLOCK), preferred_element_type=F32
         )
         kept = own_group(wide, groups)
         for s in range(seqs):
@@ -268,6 +204,392 @@
         second(step).wait_send()
 
 
+def exchange_kernel(
+    along_z, w_ref, rows_ref, taps_ref, behind_ref, ahead_ref, tail_ref, cotangent_ref,
+    out_ref, grad_ref, mixed_ref, product_ref, mix_ref, front_ref, later_ref,
+    whole, gated, gathered, turned, queries, to_a, to_b, from_a, from_b,
+    to_right, to_left, from_left, from_right, kept_right, kept_left, own, head,
+    scratch, band, low_band,
+    z_send, z_recv, up_send, up_recv, down_send, down_recv, far_send, far_recv,
+    pair_send, pair_recv, x_send, x_recv, sum_send, sum_recv, halo_send, halo_recv,
+):
+    ctx, core, x = lax.axis_index("ctx"), lax.axis_index("dp"), lax.axis_index("grp")
+    size, ring = lax.axis_size("ctx"), lax.axis_size("grp")
+    lines = size // along_z
+    y, z = ctx // along_z, ctx % along_z
+    part = w_ref.shape[0] // 2
+    total, chans = gated.shape
+    half = total // 2
+    seqs, row_count = rows_ref.shape[0], rows_ref.shape[2]
+    tiles = chans // LANES
+    groups = behind_ref.shape[0] // tiles
+
+    def at_z(step):
+        return {"ctx": y * along_z + (z + along_z + step) % along_z}
+
+    def at_y(step):
+        return {"ctx": (y + lines + step) % lines * along_z + z}
+
+    def at_x(step):
+        return {"grp": (x + ring + step) % ring}
+
+    def at_ctx(step):
+        return {"ctx": (ctx + size + step) % size}
+
+    partner = {"dp": 1 - core}
+    barrier = pltpu.get_barrier_semaphore()
+    greeted = (at_z(1), at_z(-1), at_y(1), at_y(-1), at_x(1), at_x(-1), at_ctx(1), at_ctx(-1), partner)
+    for device in greeted:
+        pl.semaphore_signal(barrier, inc=1, device_id=device, device_id_type=MESH)
+    pl.semaphore_wait(barrier, len(greeted))
+
+    def copy(src, dst, send, recv, device):
+        return pltpu.make_async_remote_copy(
+            src_ref=src, dst_ref=dst, send_sem=send, recv_sem=recv, device_id=device, device_id_type=MESH
+        )
+
+    started = []
+
+    def go(*what):
+        started.append(copy(*what))
+        started[-1].start()
+
+    def arrive(here, send, recv, device):
+        copy(here, here, send, recv, device).wait_recv()
+
+    def halo(n, src, dst, device):
+        go(src, dst, halo_send.at[n], halo_recv.at[n], device)
+
+    def halo_wait(n, here, device, edge):
+        arrive(here, halo_send.at[n], halo_recv.at[n], device)
+
+        @pl.when(ctx == edge)
+        def _():
+            here[...] = jnp.zeros(here.shape, here.dtype)
+
+    def lanes_of(i):
+        return pl.ds(pl.multiple_of(i * LANES, LANES), LANES)
+
+    def lines_of(ref, i):
+        return ref[pl.ds(pl.multiple_of(i * groups, groups), groups), :]
+
+    def block(step_y, step_z, carrier):
+        row = ((y + lines + step_y) % lines * along_z + (z + along_z + step_z) % along_z) * 2 + carrier
+        return whole.at[pl.ds(pl.multiple_of(row * part, part), part), :]
+
+    steps = [0]
+    for k in range(1, along_z // 2 + 1):
+        steps += [-k, k] if 2 * k < along_z else [-k]
+
+    def hand_over(kind, step_y, u):
+        place = kind * along_z + u
+        mine = block(step_y, steps[u], core)
+        go(mine, mine, pair_send.at[place], pair_recv.at[place], partner)
+
+    def z_turn(u):
+        mine = w_ref.at[pl.ds(pl.multiple_of(core * part, part), part), :]
+        if u > 0:
+            mine = block(0, steps[u], core)
+            arrive(mine, z_send.at[u], z_recv.at[u], at_z(1))
+        for direction in (-1, 1):
+            onward = steps[u] + direction
+            if onward in steps and (u == 0 or steps[u] * direction > 0):
+                v = steps.index(onward)
+                go(mine, block(0, steps[u], core), z_send.at[v], z_recv.at[v], at_z(-direction))
+        go(mine, block(0, steps[u], core), up_send.at[u], up_recv.at[u], at_y(1))
+        go(mine, block(0, steps[u], core), down_send.at[u], down_recv.at[u], at_y(-1))
+        if u > 0:
+            hand_over(0, 0, u)
+
+    def y_turn(u):
+        behind, ahead = block(-1, steps[u], core), block(1, steps[u], core)
+        arrive(behind, up_send.at[u], up_recv.at[u], at_y(1))
+        if u % 2 == 0:
+            go(behind, behind, far_send.at[u], far_recv.at[u], at_y(1))
+        hand_over(1, -1, u)
+        arrive(ahead, down_send.at[u], down_recv.at[u], at_y(-1))
+        if u % 2 == 1:
+            go(ahead, ahead, far_send.at[u], far_recv.at[u], at_y(-1))
+        hand_over(2, 1, u)
+
+    def far_turn(u):
+        arrive(block(2, steps[u], core), far_send.at[u], far_recv.at[u], at_y(1))
+        hand_over(3, 2, u)
+
+    pieces = [(b, s) for b in (1, 0) for s in range(seqs)]
+
+    def flat_rows(b, s):
+        return pl.ds((b * seqs + s) * BLOCK, BLOCK)
+
+    def x_start(c):
+        here = flat_rows(*pieces[c])
+        src = gated.at[here, :]
+        go(src, gathered.at[0, here, :], x_send.at[0, c], x_recv.at[0, c], at_x(1))
+        go(src, gathered.at[1, here, :], x_send.at[1, c], x_recv.at[1, c], at_x(-1))
+
+    def x_wait(slot, c):
+        arrive(gathered.at[slot, flat_rows(*pieces[c]), :], x_send.at[slot, c], x_recv.at[slot, c], at_x(1))
+
+    def x_turn(c):
+        x_wait(0, c)
+        x_wait(1, c)
+        here = flat_rows(*pieces[c])
+        slot, to = (0, at_x(1)) if c < len(pieces) // 2 else (1, at_x(-1))
+        go(gathered.at[slot, here, :], gathered.at[2, here, :], x_send.at[2, c], x_recv.at[2, c], to)
+
+    def mix_block(i, b):
+        wide = jnp.dot(band[i], window_pair(product_ref, b * BLOCK, lanes_of(i)), preferred_element_type=F32)
+        kept = own_group(wide, groups)
+        for s in range(seqs):
+            mixed = kept[:, s * LANES : (s + 1) * LANES]
+            here = slice(b * BLOCK, (b + 1) * BLOCK)
+            mixed_ref[s, here, lanes_of(i)] = mixed
+            gated[flat_rows(b, s), lanes_of(i)] = (queries[s, here, lanes_of(i)] * mixed).astype(BF)
+
+    def taps_of(i):
+        return taps_ref[:, :, lanes_of(i)]
+
+    def features_of(i, s, streams, count):
+        found = []
+        for stream in streams:
+            fill(scratch, front_ref[s, stream, :, lanes_of(i)], rows_ref[s, stream, 0:count, lanes_of(i)])
+            taps, sum_ = taps_of(i), None
+            for offset in range(taps.shape[1]):
+                start = HALO - offset
+                term = taps[stream, offset : offset + 1, :] * scratch[start : start + count, :]
+                sum_ = term if sum_ is None else sum_ + term
+            found.append(sum_)
+        return found
+
+    def forward(i, carry):
+        for s in range(seqs):
+            query, key, value = features_of(i, s, range(3), row_count)
+            queries[s, :, lanes_of(i)] = query
+            product_ref[s, BLOCK:, lanes_of(i)] = (key * value).astype(BF)
+        band_rows(lines_of(behind_ref, i), band.at[i])
+        mix_block(i, 1)
+        return carry
+
+    def forward_first(i, carry):
+        mix_block(i, 0)
+        return carry
+
+    halo(0, rows_ref.at[:, :, row_count - HALO :, :], front_ref, at_ctx(1))
+    z_turn(0)
+    halo(1, tail_ref, product_ref.at[:, 0:BLOCK, :], at_ctx(1))
+    for b in range(row_count // BLOCK):
+        for s in range(seqs):
+            turned[flat_rows(b, s), :] = cotangent_ref[s, b * BLOCK : (b + 1) * BLOCK, :]
+    for u in range(1, min(3, along_z)):
+        z_turn(u)
+    halo_wait(0, front_ref, at_ctx(1), 0)
+    lax.fori_loop(0, tiles, forward, 0)
+    x_start(0)
+    x_start(1)
+    whole[pl.ds(pl.multiple_of(ctx * 2 * part, 2 * part), 2 * part), :] = w_ref[...]
+
+    def second_half():
+        halo_wait(1, product_ref.at[:, 0:BLOCK, :], at_ctx(1), 0)
+        lax.fori_loop(0, tiles, forward_first, 0)
+        x_start(2)
+        x_start(3)
+
+    plan = []
+    for u in range(along_z + 2):
+        if 3 <= u < along_z:
+            plan.append((z_turn, u))
+        if 0 <= u - 1 < along_z and u > 0:
+            plan.append((y_turn, u - 1))
+        if 0 <= u - 2 < along_z and u > 1:
+            plan.append((far_turn, u - 2))
+        if u == min(4, along_z):
+            plan.append((second_half,))
+        if u == min(5, along_z + 1):
+            plan.append((x_turn, 0))
+        if u == min(7, along_z + 1):
+            plan.append((x_turn, 1))
+        if u == along_z:
+            plan.append((x_turn, 2))
+    plan.append((x_turn, 3))
+    if along_z < 8:
+        plan = [p for p in plan if p[0] is not x_turn] + [(x_turn, c) for c in range(4)]
+    for what, *which in plan:
+        what(*which)
+    for kind, step_y in enumerate((0, -1, 1, 2)):
+        for u in range(1 if kind == 0 else 0, along_z):
+            place = kind * along_z + u
+            arrive(block(step_y, steps[u], 1 - core), pair_send.at[place], pair_recv.at[place], partner)
+
+    wide = min(chans, 256)
+    right, left, across = (x + 1) % ring, (x + ring - 1) % ring, (x + 2) % ring
+    count = chans // wide
+
+    def columns(j):
+        return pl.ds(pl.multiple_of(j * wide, wide), wide)
+
+    def partial(owner, j):
+        rows = whole[pl.ds(pl.multiple_of(owner * chans + j * wide, wide), wide), :]
+        return lax.dot_general(turned[...], rows, (((1,), (1,)), ((), ())), preferred_element_type=F32)
+
+    def far_sums(j, carry):
+        found = partial(across, j)
+        to_a[:, columns(j)] = found[:half].astype(BF)
+        to_b[:, columns(j)] = found[half:].astype(BF)
+        return carry
+
+    def near_sums(j, carry):
+        found = partial(left, j)
+        to_left[:half, columns(j)] = found[:half].astype(BF)
+        kept_left[:, columns(j)] = found[half:]
+        found = partial(right, j)
+        kept_right[:, columns(j)] = found[:half]
+        to_right[half:, columns(j)] = found[half:].astype(BF)
+        return carry
+
+    def own_sums(j, carry):
+        own[:, columns(j)] = partial(x, j)
+        return carry
+
+    def outputs(j, carry):
+        found = None
+        for slot, owner in ((None, x), (0, left), (1, right), (2, across)):
+            rows = whole[pl.ds(pl.multiple_of(owner * chans, chans), chans), columns(j)]
+            source = gated[...] if slot is None else gathered[slot]
+            term = jnp.dot(source, rows, preferred_element_type=F32)
+            found = term if found is None else found + term
+        for b in range(row_count // BLOCK):
+            for s in range(seqs):
+                at = (b * seqs + s) * BLOCK
+                out_ref[s, b * BLOCK : (b + 1) * BLOCK, columns(j)] = found[at : at + BLOCK].astype(BF)
+        return carry
+
+    def piece(ref, at, n):
+        return ref.at[pl.ds(at + n * BLOCK, BLOCK), :]
+
+    def send_sum(n, src, dst, device):
+        go(src, dst, sum_send.at[n], sum_recv.at[n], device)
+
+    def wait_sum(n, here):
+        arrive(here, sum_send.at[n], sum_recv.at[n], at_x(1))
+
+    def relay_a(n):
+        wait_sum(n, piece(from_a, 0, n))
+        rows = slice(n * BLOCK, (n + 1) * BLOCK)
+        to_right[rows, :] = (kept_right[rows, :] + from_a[rows, :].astype(F32)).astype(BF)
+        send_sum(4 + n, piece(to_right, 0, n), piece(from_left, 0, n), at_x(1))
+
+    def relay_b(n):
+        wait_sum(2 + n, piece(from_b, 0, n))
+        rows, there = slice(n * BLOCK, (n + 1) * BLOCK), slice(half + n * BLOCK, half + (n + 1) * BLOCK)
+        to_left[there, :] = (kept_left[rows, :] + from_b[rows, :].astype(F32)).astype(BF)
+        send_sum(6 + n, piece(to_left, half, n), piece(from_right, half, n), at_x(-1))
+
+    first, second = pl.ds(0, half), pl.ds(half, half)
+    lax.fori_loop(0, count, far_sums, 0)
+    for n in range(2):
+        send_sum(n, piece(to_a, 0, n), piece(from_a, 0, n), at_x(1))
+        send_sum(2 + n, piece(to_b, 0, n), piece(from_b, 0, n), at_x(-1))
+    lax.fori_loop(0, count, near_sums, 0)
+    send_sum(8, to_left.at[first, :], from_right.at[first, :], at_x(-1))
+    relay_a(0)
+    lax.fori_loop(0, count, own_sums, 0)
+    relay_a(1)
+    send_sum(9, to_right.at[second, :], from_left.at[second, :], at_x(1))
+    relay_b(0)
+    relay_b(1)
+    for c in range(len(pieces)):
+        x_wait(2, c)
+    lax.fori_loop(0, count, outputs, 0)
+
+    def finish(b):
+        for s in range(seqs):
+            at = slice((b * seqs + s) * BLOCK, (b * seqs + s + 1) * BLOCK)
+            here = slice(b * BLOCK, (b + 1) * BLOCK)
+            found = own[at, :] + (from_left[at, :].astype(F32) + from_right[at, :].astype(F32))
+            found = found.astype(BF)
+            grad_ref[s, here, :] = found
+            mix_ref[s, here, :] = (found.astype(F32) * queries[s, here, :]).astype(BF)
+
+    wait_sum(8, from_right.at[first, :])
+    for n in range(2):
+        wait_sum(4 + n, piece(from_left, 0, n))
+    finish(0)
+    halo(2, mix_ref.at[:, 0:BLOCK, :], mix_ref.at[:, row_count:, :], at_ctx(-1))
+    wait_sum(9, from_left.at[second, :])
+    for n in range(2):
+        wait_sum(6 + n, piece(from_right, half, n))
+    finish(1)
+
+    def heads(i, carry):
+        band_rows(lines_of(ahead_ref, i), low_band, HALO)
+        low = jnp.dot(low_band[...], window_pair(mix_ref, 0, lanes_of(i)), preferred_element_type=F32)
+        pulled = own_group(low, groups, HALO)
+        for s in range(seqs):
+            here = pulled[:, s * LANES : (s + 1) * LANES]
+            key, value = features_of(i, s, (1, 2), HALO)
+            grad = grad_ref[s, 0:HALO, lanes_of(i)].astype(F32)
+            head[s, 0, :, lanes_of(i)] = (grad * mixed_ref[s, 0:HALO, lanes_of(i)]).astype(BF)
+            head[s, 1, :, lanes_of(i)] = (here * value).astype(BF)
+            head[s, 2, :, lanes_of(i)] = (here * key).astype(BF)
+        return carry
+
+    lax.fori_loop(0, tiles, heads, 0)
+    halo(3, head, later_ref, at_ctx(-1))
+    halo_wait(2, mix_ref.at[:, row_count:, :], at_ctx(-1), size - 1)
+    halo_wait(3, later_ref, at_ctx(-1), size - 1)
+    for sent in started:
+        sent.wait_send()
+
+
+def exchange(out_w, rows, short_w, lines_behind, lines_ahead, tail, grad_out):
+    seqs, row_count, chans = grad_out.shape
+    total = seqs * row_count
+    depth = out_w.shape[0] * lax.axis_size("ctx")
+    tiles = chans // LANES
+    groups = lines_behind.shape[0] // tiles
+    half = (total // 2, chans)
+    dma = pltpu.SemaphoreType.DMA
+    flops = 4 * total * depth * chans
+    padded = (seqs, row_count + BLOCK, chans)
+    edge = (seqs, 3, HALO, chans)
+    shape = jax.ShapeDtypeStruct
+    return pl.pallas_call(
+        functools.partial(exchange_kernel, ALONG_Z),
+        out_shape=[
+            shape(grad_out.shape, BF), shape(grad_out.shape, BF), shape(grad_out.shape, F32),
+            shape(padded, BF), shape(padded, BF), shape(edge, BF), shape(edge, BF),
+        ],
+        in_specs=[pl.BlockSpec(memory_space=pltpu.VMEM)] * 7,
+        out_specs=[pl.BlockSpec(memory_space=pltpu.VMEM)] * 7,
+        scratch_shapes=[
+            pltpu.VMEM((depth, chans), BF),
+            pltpu.VMEM((total, chans), BF),
+            pltpu.VMEM((3, total, chans), BF),
+            pltpu.VMEM((total, chans), BF),
+            pltpu.VMEM((seqs, row_count, chans), F32),
+        ]
+        + [pltpu.VMEM(half, BF)] * 4
+        + [pltpu.VMEM((total, chans), BF)] * 4
+        + [pltpu.VMEM(half, F32)] * 2
+        + [
+            pltpu.VMEM((total, chans), F32),
+            pltpu.VMEM(edge, BF),
+            pltpu.VMEM((row_count + HALO, LANES), F32),
+            pltpu.VMEM((tiles, groups * BLOCK, 2 * BLOCK), BF),
+            pltpu.VMEM((groups * HALO, 2 * BLOCK), BF),
+        ]
+        + [dma((ALONG_Z,))] * 8
+        + [dma((4 * ALONG_Z,))] * 2
+        + [dma((3, 4))] * 2
+        + [dma((10,))] * 2
+        + [dma((4,))] * 2,
+        cost_estimate=pl.CostEstimate(flops=flops, bytes_accessed=8 * total * chans, transcendentals=0),
+        compiler_params=pltpu.CompilerParams(
+            collective_id=2, has_side_effects=True, vmem_limit_bytes=58 << 20
+        ),
+    )(out_w, rows, short_w, lines_behind, lines_ahead, tail, grad_out)
+
+
 def tiled(kernel, ins, outs, scratch, arrays, tiles, flops=0):
     read = sum(math.prod(a.shape) * a.dtype.itemsize for a in arrays)
     return pl.pallas_call(
@@ -301,12 +623,10 @@
     lines_spec = ((groups, 2 * BLOCK), lambda i: (i, 0))
     edge_spec = ((seqs, BLOCK, LANES), lane3)
     full_spec = ((seqs, row_count, LANES), lane3)
-    full = (seqs, row_count, chans)
     line_rows = pltpu.VMEM((row_count + HALO, LANES), F32)
-    long_rows = pltpu.VMEM((seqs, row_count + BLOCK, LANES), BF)
+    padded_spec = ((seqs, row_count + BLOCK, LANES), lane3)
     bands = pltpu.VMEM((groups * BLOCK, 2 * BLOCK), BF)
 
-    front = from_behind(rows[:, :, row_count - HALO :], "ctx", 1)
     tail = tiled(
         tail_kernel,
         [
@@ -319,63 +639,40 @@
         (rows, rows, short_w),
         tiles,
     )[0]
-    behind = from_behind(tail, "ctx", 1)
-    gated, mixed, product = tiled(
-        forward_kernel,
-        [front_spec, rows_spec, taps_spec, lines_spec, edge_spec],
-        [(*full_spec, full, BF), (*full_spec, full, F32), (*full_spec, full, BF)],
-        [line_rows, long_rows, pltpu.VMEM((seqs, row_count, LANES), F32), bands],
-        (front, rows, short_w, lines_behind, behind),
-        tiles,
+    block_out, cotangent, mixed, product, mix, front, later = exchange(
+        out_w, rows, short_w, lines_behind, lines_ahead, tail, grad_out
     )
-
-    whole_w = lax.all_gather(out_w, "ctx", axis=0, tiled=True)
-    whole_gated = lax.all_gather(gated, "grp", axis=2, tiled=True)
-    flat_gated = whole_gated.reshape(seqs * row_count, whole_gated.shape[2])
-    block_out = jnp.dot(flat_gated, whole_w, preferred_element_type=F32).astype(BF).reshape(full)
-    input_part = lax.dot_general(
-        grad_out.reshape(seqs * row_count, chans), whole_w, (((1,), (1,)), ((), ())), preferred_element_type=F32
-    )
-    summed = lax.psum_scatter(input_part, "grp", scatter_dimension=1, tiled=True)
-    cotangent = summed.astype(BF).reshape(full)
-
-    mix, head = tiled(
-        mix_kernel,
-        [full_spec, front_spec, rows_spec, taps_spec, lines_spec, full_spec],
-        [(*full_spec, full, BF), (*front_spec, (seqs, 3, HALO, chans), BF)],
-        [line_rows, bands],
-        (cotangent, front, rows, short_w, lines_ahead, mixed),
-        tiles,
-    )
-    ahead = from_behind(mix[:, :BLOCK], "ctx", -1)
-    later = from_behind(head, "ctx", -1)
     filter_part = tiled(
         filter_kernel,
-        [full_spec, full_spec, edge_spec],
+        [full_spec, padded_spec],
         [((groups, LANES), lambda i: (i, 0), (groups_here, taps), F32)],
-        [long_rows],
-        (mix, product, behind),
+        [],
+        (mix, product),
         tiles,
     )[0]
     grad, short_part = tiled(
         backward_kernel,
-        [full_spec, front_spec, rows_spec, taps_spec, lines_spec, full_spec, full_spec, edge_spec, front_spec],
+        [full_spec, front_spec, rows_spec, taps_spec, lines_spec, full_spec, padded_spec, front_spec],
         [(*rows_spec, rows.shape, BF), ((1, HALO, LANES), lambda i: (i, 0, 0), (tiles, HALO, LANES), F32)],
-        [line_rows, long_rows, pltpu.VMEM((seqs, row_count, LANES), F32), line_rows, bands],
-        (cotangent, front, rows, short_w, lines_ahead, mixed, mix, ahead, later),
+        [line_rows, pltpu.VMEM((seqs, row_count, LANES), F32), line_rows, bands],
+        (cotangent, front, rows, short_w, lines_ahead, mixed, mix, later),
         tiles,
     )
 
-    pieces = 8
+    pieces = ALONG_Z
     packed = jnp.concatenate([filter_part, short_part.reshape(tiles * HALO, LANES)], axis=0)
     depth = packed.shape[0] // pieces
     piece = (depth, LANES)
+    peers = 2 * (lax.axis_size("ctx") // pieces)
     sums = pl.pallas_call(
         reduce_kernel,
         out_shape=jax.ShapeDtypeStruct((pieces, *piece), F32),
         in_specs=[pl.BlockSpec(memory_space=pltpu.VMEM)],
         out_specs=pl.BlockSpec(memory_space=pltpu.VMEM),
-        scratch_shapes=[pltpu.VMEM((pieces, *piece), F32), pltpu.VMEM(piece, F32)] * 2
+        scratch_shapes=[
+            pltpu.VMEM((pieces, *piece), F32), pltpu.VMEM(piece, F32),
+            pltpu.VMEM((peers, *piece), F32), pltpu.VMEM(piece, F32),
+        ]
         + [pltpu.SemaphoreType.DMA((8,))] * 6,
         compiler_params=pltpu.CompilerParams(collective_id=1, has_side_effects=True),
     )(packed.reshape(pieces, *piece)).reshape(packed.shape)

time: 319 us -> 178 us (0.56)
  waiting for transfers between devices: 204 us -> 0 us
  Pallas kernels: 59.8 us -> 162 us
  matrix products: 20.3 us -> 0 us
  between operations: 13.9 us -> 0.75 us
  starting transfers between devices: 7.89 us -> 0 us
    all_gather x2 -> x0, waiting for transfers between devices: 142 us -> none  [the longest x1 104 us: shards(): whole_w = lax.all_gather(out_w, 'ctx', axis=0, tiled=True)]
    pallas_call x0 -> x1, Pallas kernels: none -> 118 us  [exchange(): pl.pallas_call(functools.partial(exchange_kernel, ALONG_Z), out_shape=[sh...]
    reduce_scatter x1 -> x0, waiting for transfers between devices: 50.1 us -> none  [shards(): lax.psum_scatter(input_part, 'grp', scatter_dimension=1, tiled=True)]
    dot_general x2 -> x0, matrix products: 20.3 us -> none  [the longest x1 10.2 us: shards(): jnp.dot(flat_gated, whole_w, preferred_element_type=F32).astype(BF)]
    pallas_call x5 -> x3, Pallas kernels: 36.7 us -> 20.9 us  [tiled(): pl.pallas_call(kernel, grid=(tiles,), in_specs=[pl.BlockSpec(block, index...]
    ppermute x4 -> x0, waiting for transfers between devices: 10.6 us -> none  [from_behind(): return lax.ppermute(block, axis, route)]
    ppermute x4 -> x0, starting transfers between devices: 7.77 us -> none  [from_behind(): return lax.ppermute(block, axis, route)]
    unnamed x22 -> x27, local copies, waits for them, and re-layouts: 6.46 us -> 8.86 us
  transfers between devices with their start and end apart: 7 -> 0, of which waited for: 4 -> 0; matrix products, arithmetic and copies ran while one was open for 4% -> 0% of each run, Pallas kernels for 7% -> 0%
where the time goes in v3:
time: 178 us
  Pallas kernels  162 us (91%)
  local copies, waits for them, and re-layouts  12 us (7%)
  other arithmetic  2.71 us (2%)
    pallas_call x1, Pallas kernels, exchange(): pl.pallas_call(functools.partial(exchange_kernel, ALONG_Z), out_shape=[sh...  118 us
    pallas_call x1, Pallas kernels, shards(): pl.pallas_call(reduce_kernel, out_shape=jax.ShapeDtypeStruct((pieces, *pi...  22.8 us
    pallas_call x3, Pallas kernels, tiled(): pl.pallas_call(kernel, grid=(tiles,), in_specs=[pl.BlockSpec(block, index...  20.9 us
    unnamed x27, local copies, waits for them, and re-layouts  8.86 us

profile of v3, /device:TPU:1, one launch (start us, length us, event | category | flops | bytes accessed | tf_op | source)
XLA Modules:
  0.0 177.6 jit_solution(5066968899193681008)
XLA Ops:
  0.6 0.8 rev.6
  1.4 1.4 pad_convert_fusion
  2.8 1.9 %copy-done = bf16[2,256,3,1024]{3,1,2,0:T(8,128)(2,1)S(1)} copy-done((bf16[2,256,3,1024]{3,1,2,0:T(8,128)(2,1)S(1)}, bf16[2,256,3,1024]{3,1,2,0:T(8,128)(2,1)}, u32[]{:S(2)}) %copy-start) | copy-done | bytes 3145752
  4.7 0.8 copy-done.8
  5.5 1.3 shard_map.84.tail_ref
  6.9 0.0 copy-start.6
  6.9 0.8 copy-done.6
  7.7 118.4 %shard_map.85 = (bf16[2,256,1024]{2,1,0:T(8,128)(2,1)}, bf16[2,256,1024]{2,1,0:T(8,128)(2,1)}, f32[2,256,1024]{2,1,0:T(8,128)}, bf16[2,384,1024]{2,1,0:T(8,128)(...) custom-call(bf16[128,1024]{1,0:T(8,128)(2,1)} %w_ref.1, ...), custom_call_target="tpu_custom_call" | custom-call | flops 8589934592 | bytes 4194304 | tf_op jit(solution)/shard_map/pallas_call | solution.py:556
  126.1 0.0 copy-start.1
  126.1 1.4 copy-done.1
  127.5 1.4 copy-done.4
  128.9 5.7 %shard_map.87 = f32[64,128]{1,0:T(8,128)S(1)} custom-call(bf16[2,384,1024]{2,1,0:T(8,128)(2,1)S(1)} %copy-done.1, bf16[2,384,1024]{2,1,0:T(8,128)(2,1)S(1)} %copy-done.4), custom_call_target="tpu_custom_call" | custom-call | bytes 3145728 | tf_op jit(solution)/shard_map/pallas_call | solution.py:595
  134.6 0.0 copy-done.7
  134.7 1.6 copy-done.3
  136.3 13.9 %shard_map.86 = (bf16[2,3,256,1024]{3,2,1,0:T(8,128)(2,1)}, f32[8,16,128]{2,1,0:T(8,128)S(1)}) custom-call(bf16[2,256,1024]{2,1,0:T(8,128)(2,1)S(1)} %copy-done.5, bf16[2,3,16,1024]{3,2,1,0:T(8,128)(2,1)S(1)} %copy-done.10, bf16[2,3,256,1024]{3,2,1,0:T(8,128)(2,1)} %bitcast.10, f32[3,3,1024]{2,1,0:T(4,128)S(1)} %copy-done.9, f32[64,256]{1,0:T(8,128)S(1)} %copy-done.7, ...), custom_call_target="tpu_custom_call" | custom-call | bytes 8359936 | tf_op jit(solution)/shard_map/pallas_call | solution.py:595
  150.2 0.6 pad_maximum_fusion
  150.8 22.8 %shard_map.88 = f32[8,24,128]{2,1,0:T(8,128)} custom-call(f32[8,24,128]{2,1,0:T(8,128)} %bitcast.14), custom_call_target="tpu_custom_call" | custom-call | tf_op jit(solution)/shard_map/pallas_call | solution.py:667
  173.6 0.8 slice.12
  174.4 0.8 slice.13
  175.3 0.1 rev.7
  175.3 0.6 broadcast_multiply_fusion
  176.0 0.6 div.21
  176.6 0.0 copy-done.12
  176.6 1.0 copy.15
  (17 shorter events, 0.0 us)
Async XLA Ops:
  2.8 1.9 %copy-start = (bf16[2,256,3,1024]{3,1,2,0:T(8,128)(2,1)S(1)}, bf16[2,256,3,1024]{3,1,2,0:T(8,128)(2,1)}, u32[]{:S(2)}) copy-start(bf16[2,256,3,1024]{3,1,2,0:T(8,128)(2,1)} %param.5) | copy-start | bytes 9437188
  4.7 0.8 copy-start.8
  6.9 0.8 copy-start.6
  7.7 127.0 %copy-start.7 = (f32[64,256]{1,0:T(8,128)S(1)}, f32[64,256]{1,0:T(8,128)}, u32[]{:S(2)}) copy-start(f32[64,256]{1,0:T(8,128)} %get-tuple-element.22.ahead_ref.lines_ref) | copy-start | bytes 196612
  7.7 127.0 %copy-start.9 = (f32[3,3,1024]{2,1,0:T(4,128)S(1)}, f32[3,3,1024]{2,1,0:T(4,128)}, u32[]{:S(2)}) copy-start(f32[3,3,1024]{2,1,0:T(4,128)} %taps_ref.5) | copy-start | bytes 110596
  126.1 1.4 copy-start.1
  127.5 1.4 copy-start.4
  128.9 5.8 %copy-start.2 = (bf16[2,384,1024]{2,1,0:T(8,128)(2,1)S(1)}, bf16[2,384,1024]{2,1,0:T(8,128)(2,1)}, u32[]{:S(2)}) copy-start(bf16[2,384,1024]{2,1,0:T(8,128)(2,1)} %get-tuple-element.17.padded_ref.mix_ref) | copy-start | bytes 4718596
  128.9 5.8 %copy-start.5 = (bf16[2,256,1024]{2,1,0:T(8,128)(2,1)S(1)}, bf16[2,256,1024]{2,1,0:T(8,128)(2,1)}, u32[]{:S(2)}) copy-start(bf16[2,256,1024]{2,1,0:T(8,128)(2,1)} %get-tuple-element.14.cotangent_ref) | copy-start | bytes 3145732
  128.9 5.8 %copy-start.10 = (bf16[2,3,16,1024]{3,2,1,0:T(8,128)(2,1)S(1)}, bf16[2,3,16,1024]{3,2,1,0:T(8,128)(2,1)}, u32[]{:S(2)}) copy-start(bf16[2,3,16,1024]{3,2,1,0:T(8,128)(2,1)} %get-tuple-element.15.front_ref) | copy-start | bytes 589828
  128.9 5.8 %copy-start.11 = (bf16[2,3,16,1024]{3,2,1,0:T(8,128)(2,1)S(1)}, bf16[2,3,16,1024]{3,2,1,0:T(8,128)(2,1)}, u32[]{:S(2)}) copy-start(bf16[2,3,16,1024]{3,2,1,0:T(8,128)(2,1)} %get-tuple-element.18.next_ref) | copy-start | bytes 589828
  134.7 1.6 copy-start.3
  136.3 40.3 %copy-start.12 = (bf16[2,256,1024]{2,1,0:T(8,128)(2,1)S(1)}, bf16[2,256,1024]{2,1,0:T(8,128)(2,1)}, u32[]{:S(2)}) copy-start(bf16[2,256,1024]{2,1,0:T(8,128)(2,1)} %get-tuple-element.28) | copy-start | bytes 3145732

commit v4 on v3

--- a/solution.py
+++ b/solution.py
@@ -31,6 +31,17 @@
     return total
 
 
+def ahead_lines(filters):
+    return jnp.concatenate([filters.astype(F32), jnp.zeros(filters.shape, F32)], axis=1)
+
+
+def behind_lines(filters):
+    taps = filters.shape[1]
+    row = lax.broadcasted_iota(jnp.int32, (taps, 2 * BLOCK), 0)
+    column = lax.broadcasted_iota(jnp.int32, (taps, 2 * BLOCK), 1)
+    return jnp.dot(filters, (row + column == BLOCK).astype(BF), preferred_element_type=F32)
+
+
 def band_rows(lines, band, count=BLOCK):
     groups = lines.shape[0]
     for g in range(groups):
@@ -58,49 +69,43 @@
     )
 
 
-def tail_kernel(front_ref, rows_ref, taps_ref, out_ref, scratch):
-    for s in range(rows_ref.shape[0]):
-        found = []
-        for stream in (1, 2):
-            fill(scratch, front_ref[s, stream], rows_ref[s, stream])
-            found.append(feature(scratch, taps_ref, stream, BLOCK))
-        out_ref[s] = (found[0] * found[1]).astype(BF)
-
-
-def filter_kernel(mix_ref, padded_ref, sums_ref):
-    seqs, row_count = padded_ref.shape[0], padded_ref.shape[1] - BLOCK
+def filter_sums(mix_ref, product_ref, sums_ref):
+    seqs, row_count = product_ref.shape[0], product_ref.shape[1] - BLOCK
     groups = sums_ref.shape[0]
-    blocks = row_count // BLOCK
-    rows = lax.broadcasted_iota(jnp.int32, (BLOCK, BLOCK), 0)
-    columns = lax.broadcasted_iota(jnp.int32, (BLOCK, BLOCK), 1)
-    upturn = (rows + columns == BLOCK - 1).astype(BF)
+    rows = lax.broadcasted_iota(jnp.int32, (2 * BLOCK, 2 * BLOCK), 0)
+    columns = lax.broadcasted_iota(jnp.int32, (2 * BLOCK, 2 * BLOCK), 1)
+    upturn = (rows + columns == 2 * BLOCK - 1).astype(BF)
     parts, wins = [], []
     for s in range(seqs):
-        for b in range(blocks):
+        for b in range(row_count // BLOCK):
             parts.append(mix_ref[s, b * BLOCK : (b + 1) * BLOCK, :])
-            wins.append(padded_ref[s, b * BLOCK : (b + 2) * BLOCK, :])
-    grads = jnp.dot(upturn, jnp.concatenate(parts, axis=1), preferred_element_type=F32)
-    windows = jnp.concatenate(wins, axis=1)
+            wins.append(product_ref[s, b * BLOCK : (b + 2) * BLOCK, :])
+    grads = jnp.concatenate(parts, axis=1)
+    windows = jnp.dot(upturn, jnp.concatenate(wins, axis=1), preferred_element_type=F32).astype(BF)
     owner = group_of_lane(grads.shape, groups)
     stacked = jnp.concatenate(
-        [jnp.where(owner == g, grads, 0.0).astype(BF) for g in range(groups)], axis=0
+        [jnp.where(owner == g, grads.astype(F32), 0.0).astype(BF) for g in range(groups)], axis=0
     )
     lags = lax.dot_general(
         stacked, windows, (((1,), (1,)), ((), ())), preferred_element_type=F32
     )
+    found = []
     for g in range(groups):
         turned = pltpu.roll(lags[g * BLOCK : (g + 1) * BLOCK], 0, 1, stride=1, stride_axis=0)
-        sums_ref[g : g + 1, :] = jnp.sum(turned[:, BLOCK:], axis=0, keepdims=True)
+        found.append(jnp.sum(turned, axis=0, keepdims=True))
+    sums_ref[...] = pltpu.roll(jnp.concatenate(found, axis=0), BLOCK + 1, 1)[:, :BLOCK]
 
 
 def backward_kernel(
-    cotangent_ref, front_ref, rows_ref, taps_ref, lines_ref, mixed_ref,
-    padded_ref, next_ref, grad_ref, short_ref, scratch, pulled, later, band,
+    cotangent_ref, front_ref, rows_ref, taps_ref, filters_ref, mixed_ref,
+    padded_ref, product_ref, next_ref, grad_ref, short_ref, sums_ref, scratch, pulled, later, band,
 ):
     seqs, row_count = rows_ref.shape[0], rows_ref.shape[2]
-    groups = lines_ref.shape[0]
+    groups = sums_ref.shape[0]
     taps = taps_ref.shape[1]
-    band_rows(lines_ref[...], band)
+    filter_sums(padded_ref, product_ref, sums_ref)
+    first = pl.multiple_of(pl.program_id(0) * groups, groups)
+    band_rows(ahead_lines(filters_ref[pl.ds(first, groups), :]), band)
     for b in range(row_count // BLOCK):
         wide = jnp.dot(
             band[...], window_pair(padded_ref, b * BLOCK), preferred_element_type=F32
@@ -108,7 +113,7 @@
         kept = own_group(wide, groups)
         for s in range(seqs):
             pulled[s, b * BLOCK : (b + 1) * BLOCK, :] = kept[:, s * LANES : (s + 1) * LANES]
-    short_ref[...] = jnp.zeros_like(short_ref)
+    sums = [None] * (3 * taps)
     for s in range(seqs):
         for stream in range(3):
             if stream == 0:
@@ -126,86 +131,107 @@
                 term = taps_ref[stream, offset : offset + 1, :] * later[offset : offset + row_count, :]
                 total = term if total is None else total + term
                 at = HALO - offset
+                found = jnp.sum(grad * scratch[at : at + row_count, :], axis=0, keepdims=True)
                 row = stream * taps + offset
-                short_ref[0, row : row + 1, :] += jnp.sum(
-                    grad * scratch[at : at + row_count, :], axis=0, keepdims=True
-                )
+                sums[row] = found if sums[row] is None else sums[row] + found
             grad_ref[s, stream] = total.astype(BF)
-
-
-def reduce_kernel(x_ref, o_ref, zbuf, part, ybuf, whole, zs, zr, ys, yr, os, orr):
-    pieces = x_ref.shape[0]
+    short_ref[...] = jnp.zeros_like(short_ref)
+    for row in range(3 * taps):
+        short_ref[0, row : row + 1, :] = sums[row]
+
+
+def reduce_kernel(
+    along_z, scales, filter_ref, short_ref, filter_out, short_out,
+    packed, mine_of, part, gathered, whole, result, zs, zr, ys, yr, os, orr,
+):
     me, core = lax.axis_index("ctx"), lax.axis_index("dp")
-    line, place = me // pieces, me % pieces
-    lines = lax.axis_size("ctx") // pieces
+    line, place = me // along_z, me % along_z
+    lines = lax.axis_size("ctx") // along_z
     peers = lines * 2
     mine = line * 2 + core
+    depth = packed.shape[0] // peers
+    tiles, width = short_ref.shape[0], packed.shape[0] // short_ref.shape[0]
+    groups = width - short_ref.shape[1]
 
     def along(step):
-        return {"ctx": line * pieces + (place + step) % pieces}
+        return {"ctx": line * along_z + (place + step) % along_z}
 
     def across(step):
         other = (mine + step) % peers
-        return {"ctx": (other // 2) * pieces + place, "dp": other % 2}
+        return {"ctx": (other // 2) * along_z + place, "dp": other % 2}
 
     barrier = pltpu.get_barrier_semaphore()
-    for step in range(1, pieces):
+    for step in range(1, along_z):
         pl.semaphore_signal(barrier, inc=1, device_id=along(step), device_id_type=MESH)
     for step in range(1, peers):
         pl.semaphore_signal(barrier, inc=1, device_id=across(step), device_id_type=MESH)
-    pl.semaphore_wait(barrier, pieces + peers - 2)
+    for k in range(tiles):
+        packed[k * width : k * width + groups, :] = filter_ref[k * groups : (k + 1) * groups, :]
+        packed[k * width + groups : (k + 1) * width, :] = short_ref[k]
+    pl.semaphore_wait(barrier, along_z + peers - 2)
+
+    def rows_of(piece):
+        return pl.ds(pl.multiple_of(piece * depth, depth), depth)
 
     def first(step):
         return pltpu.make_async_remote_copy(
-            src_ref=x_ref.at[(place + step) % pieces], dst_ref=zbuf.at[place],
+            src_ref=packed.at[rows_of((mine + step) % peers), :], dst_ref=mine_of.at[mine],
             send_sem=zs.at[step], recv_sem=zr.at[step],
+            device_id=across(step), device_id_type=MESH,
+        )
+
+    def second(step):
+        return pltpu.make_async_remote_copy(
+            src_ref=part, dst_ref=gathered.at[place], send_sem=ys.at[step], recv_sem=yr.at[step],
             device_id=along(step), device_id_type=MESH,
         )
 
-    def second(step):
+    def third(step):
         return pltpu.make_async_remote_copy(
-            src_ref=part, dst_ref=ybuf.at[mine], send_sem=ys.at[step], recv_sem=yr.at[step],
+            src_ref=whole, dst_ref=result.at[rows_of(mine), :], send_sem=os.at[step], recv_sem=orr.at[step],
             device_id=across(step), device_id_type=MESH,
         )
 
-    def third(step):
-        return pltpu.make_async_remote_copy(
-            src_ref=whole, dst_ref=o_ref.at[place], send_sem=os.at[step], recv_sem=orr.at[step],
-            device_id=along(step), device_id_type=MESH,
-        )
-
-    for step in range(1, pieces):
+    for step in range(1, peers):
         first(step).start()
-    zbuf[place] = x_ref[place]
-    for step in range(1, pieces):
+    mine_of[mine] = packed[rows_of(mine), :]
+    for step in range(1, peers):
         first(step).wait_recv()
-    total = zbuf[0]
-    for k in range(1, pieces):
-        total = total + zbuf[k]
+    total = mine_of[0]
+    for k in range(1, peers):
+        total = total + mine_of[k]
     part[...] = total
+    for step in range(1, along_z):
+        second(step).start()
+    gathered[place] = total
+    for step in range(1, along_z):
+        second(step).wait_recv()
+    total = gathered[0]
+    for k in range(1, along_z):
+        total = total + gathered[k]
+    whole[...] = total
     for step in range(1, peers):
-        second(step).start()
-    ybuf[mine] = total
+        third(step).start()
+    result[rows_of(mine), :] = total
     for step in range(1, peers):
-        second(step).wait_recv()
-    total = ybuf[0]
-    for k in range(1, peers):
-        total = total + ybuf[k]
-    whole[...] = total
-    for step in range(1, pieces):
-        third(step).start()
-    o_ref[place] = total
-    for step in range(1, pieces):
         third(step).wait_recv()
-    for step in range(1, pieces):
+    taps = short_out.shape[1]
+    for k in range(tiles):
+        at = k * width
+        filter_out[k * groups : (k + 1) * groups, :] = result[at : at + groups, :] * scales[0]
+        at += groups
+        for stream in range(3):
+            rows = result[at + stream * taps : at + (stream + 1) * taps, :]
+            short_out[stream, :, k * LANES : (k + 1) * LANES] = rows * scales[1]
+    for step in range(1, peers):
         first(step).wait_send()
         third(step).wait_send()
-    for step in range(1, peers):
+    for step in range(1, along_z):
         second(step).wait_send()
 
 
 def exchange_kernel(
-    along_z, w_ref, rows_ref, taps_ref, behind_ref, ahead_ref, tail_ref, cotangent_ref,
+    along_z, w_ref, rows_ref, taps_ref, filters_ref, cotangent_ref,
     out_ref, grad_ref, mixed_ref, product_ref, mix_ref, front_ref, later_ref,
     whole, gated, gathered, turned, queries, to_a, to_b, from_a, from_b,
     to_right, to_left, from_left, from_right, kept_right, kept_left, own, head,
@@ -222,7 +248,7 @@
     half = total // 2
     seqs, row_count = rows_ref.shape[0], rows_ref.shape[2]
     tiles = chans // LANES
-    groups = behind_ref.shape[0] // tiles
+    groups = filters_ref.shape[0] // tiles
 
     def at_z(step):
         return {"ctx": y * along_z + (z + along_z + step) % along_z}
@@ -278,8 +304,10 @@
         return whole.at[pl.ds(pl.multiple_of(row * part, part), part), :]
 
     steps = [0]
+    for k in range(1, along_z // 2):
+        steps.append(k)
     for k in range(1, along_z // 2 + 1):
-        steps += [-k, k] if 2 * k < along_z else [-k]
+        steps.insert(2 if k == 1 else len(steps), -k)
 
     def hand_over(kind, step_y, u):
         place = kind * along_z + u
@@ -349,10 +377,14 @@
     def taps_of(i):
         return taps_ref[:, :, lanes_of(i)]
 
-    def features_of(i, s, streams, count):
+    def features_of(i, s, streams, count, at=0):
         found = []
         for stream in streams:
-            fill(scratch, front_ref[s, stream, :, lanes_of(i)], rows_ref[s, stream, 0:count, lanes_of(i)])
+            if at == 0:
+                before = front_ref[s, stream, :, lanes_of(i)]
+            else:
+                before = rows_ref[s, stream, at - HALO : at, lanes_of(i)]
+            fill(scratch, before, rows_ref[s, stream, at : at + count, lanes_of(i)])
             taps, sum_ = taps_of(i), None
             for offset in range(taps.shape[1]):
                 start = HALO - offset
@@ -361,12 +393,24 @@
             found.append(sum_)
         return found
 
+    def features(i, at, count):
+        for s in range(seqs):
+            query, key, value = features_of(i, s, range(3), count, at)
+            queries[s, at : at + count, lanes_of(i)] = query
+            product_ref[s, BLOCK + at : BLOCK + at + count, lanes_of(i)] = (key * value).astype(BF)
+
+    last = row_count - BLOCK
+
+    def tails(i, carry):
+        features(i, last, BLOCK)
+        return carry
+
+    def bands(i, carry):
+        band_rows(behind_lines(lines_of(filters_ref, i)), band.at[i])
+        return carry
+
     def forward(i, carry):
-        for s in range(seqs):
-            query, key, value = features_of(i, s, range(3), row_count)
-            queries[s, :, lanes_of(i)] = query
-            product_ref[s, BLOCK:, lanes_of(i)] = (key * value).astype(BF)
-        band_rows(lines_of(behind_ref, i), band.at[i])
+        features(i, 0, last)
         mix_block(i, 1)
         return carry
 
@@ -376,7 +420,9 @@
 
     halo(0, rows_ref.at[:, :, row_count - HALO :, :], front_ref, at_ctx(1))
     z_turn(0)
-    halo(1, tail_ref, product_ref.at[:, 0:BLOCK, :], at_ctx(1))
+    lax.fori_loop(0, tiles, tails, 0)
+    halo(1, product_ref.at[:, row_count:, :], product_ref.at[:, 0:BLOCK, :], at_ctx(1))
+    lax.fori_loop(0, tiles, bands, 0)
     for b in range(row_count // BLOCK):
         for s in range(seqs):
             turned[flat_rows(b, s), :] = cotangent_ref[s, b * BLOCK : (b + 1) * BLOCK, :]
@@ -402,17 +448,16 @@
             plan.append((y_turn, u - 1))
         if 0 <= u - 2 < along_z and u > 1:
             plan.append((far_turn, u - 2))
-        if u == min(4, along_z):
+        if u == min(3, along_z):
             plan.append((second_half,))
         if u == min(5, along_z + 1):
             plan.append((x_turn, 0))
-        if u == min(7, along_z + 1):
+        if u == min(6, along_z + 1):
             plan.append((x_turn, 1))
         if u == along_z:
             plan.append((x_turn, 2))
-    plan.append((x_turn, 3))
     if along_z < 8:
-        plan = [p for p in plan if p[0] is not x_turn] + [(x_turn, c) for c in range(4)]
+        plan = [p for p in plan if p[0] is not x_turn] + [(x_turn, c) for c in range(3)]
     for what, *which in plan:
         what(*which)
     for kind, step_y in enumerate((0, -1, 1, 2)):
@@ -486,6 +531,7 @@
 
     first, second = pl.ds(0, half), pl.ds(half, half)
     lax.fori_loop(0, count, far_sums, 0)
+    x_turn(3)
     for n in range(2):
         send_sum(n, piece(to_a, 0, n), piece(from_a, 0, n), at_x(1))
         send_sum(2 + n, piece(to_b, 0, n), piece(from_b, 0, n), at_x(-1))
@@ -521,7 +567,7 @@
     finish(1)
 
     def heads(i, carry):
-        band_rows(lines_of(ahead_ref, i), low_band, HALO)
+        band_rows(ahead_lines(lines_of(filters_ref, i)), low_band, HALO)
         low = jnp.dot(low_band[...], window_pair(mix_ref, 0, lanes_of(i)), preferred_element_type=F32)
         pulled = own_group(low, groups, HALO)
         for s in range(seqs):
@@ -541,12 +587,12 @@
         sent.wait_send()
 
 
-def exchange(out_w, rows, short_w, lines_behind, lines_ahead, tail, grad_out):
+def exchange(out_w, rows, short_w, medium_h, grad_out):
     seqs, row_count, chans = grad_out.shape
     total = seqs * row_count
     depth = out_w.shape[0] * lax.axis_size("ctx")
     tiles = chans // LANES
-    groups = lines_behind.shape[0] // tiles
+    groups = medium_h.shape[0] // tiles
     half = (total // 2, chans)
     dma = pltpu.SemaphoreType.DMA
     flops = 4 * total * depth * chans
@@ -559,7 +605,7 @@
             shape(grad_out.shape, BF), shape(grad_out.shape, BF), shape(grad_out.shape, F32),
             shape(padded, BF), shape(padded, BF), shape(edge, BF), shape(edge, BF),
         ],
-        in_specs=[pl.BlockSpec(memory_space=pltpu.VMEM)] * 7,
+        in_specs=[pl.BlockSpec(memory_space=pltpu.VMEM)] * 5,
         out_specs=[pl.BlockSpec(memory_space=pltpu.VMEM)] * 7,
         scratch_shapes=[
             pltpu.VMEM((depth, chans), BF),
@@ -587,7 +633,7 @@
         compiler_params=pltpu.CompilerParams(
             collective_id=2, has_side_effects=True, vmem_limit_bytes=58 << 20
         ),
-    )(out_w, rows, short_w, lines_behind, lines_ahead, tail, grad_out)
+    )(out_w, rows, short_w, medium_h, grad_out)
 
 
 def tiled(kernel, ins, outs, scratch, arrays, tiles, flops=0):
@@ -612,77 +658,58 @@
     groups = groups_here // tiles
     rows = jnp.swapaxes(projected, 1, 2)
 
-    lines_behind = jnp.pad(medium_h[:, ::-1].astype(F32), ((0, 0), (1, 2 * BLOCK - taps - 1)))
-    lines_ahead = jnp.pad(medium_h.astype(F32), ((0, 0), (0, 2 * BLOCK - taps)))
-
     lane3 = lambda i: (0, 0, i)
     lane4 = lambda i: (0, 0, 0, i)
     front_spec = ((seqs, 3, HALO, LANES), lane4)
     rows_spec = ((seqs, 3, row_count, LANES), lane4)
     taps_spec = ((3, short_w.shape[1], LANES), lane3)
-    lines_spec = ((groups, 2 * BLOCK), lambda i: (i, 0))
-    edge_spec = ((seqs, BLOCK, LANES), lane3)
+    filters_spec = ((groups_here, taps), lambda i: (0, 0))
     full_spec = ((seqs, row_count, LANES), lane3)
     line_rows = pltpu.VMEM((row_count + HALO, LANES), F32)
     padded_spec = ((seqs, row_count + BLOCK, LANES), lane3)
     bands = pltpu.VMEM((groups * BLOCK, 2 * BLOCK), BF)
 
-    tail = tiled(
-        tail_kernel,
+    block_out, cotangent, mixed, product, mix, front, later = exchange(
+        out_w, rows, short_w, medium_h, grad_out
+    )
+    grad, short_part, filter_part = tiled(
+        backward_kernel,
+        [full_spec, front_spec, rows_spec, taps_spec, filters_spec, full_spec, padded_spec, padded_spec, front_spec],
         [
-            ((seqs, 3, HALO, LANES), lambda i: (0, 0, (row_count - BLOCK) // HALO - 1, i)),
-            ((seqs, 3, BLOCK, LANES), lambda i: (0, 0, row_count // BLOCK - 1, i)),
-            taps_spec,
+            (*rows_spec, rows.shape, BF),
+            ((1, HALO, LANES), lambda i: (i, 0, 0), (tiles, HALO, LANES), F32),
+            ((groups, LANES), lambda i: (i, 0), (groups_here, taps), F32),
         ],
-        [(*edge_spec, (seqs, BLOCK, chans), BF)],
-        [line_rows],
-        (rows, rows, short_w),
-        tiles,
-    )[0]
-    block_out, cotangent, mixed, product, mix, front, later = exchange(
-        out_w, rows, short_w, lines_behind, lines_ahead, tail, grad_out
-    )
-    filter_part = tiled(
-        filter_kernel,
-        [full_spec, padded_spec],
-        [((groups, LANES), lambda i: (i, 0), (groups_here, taps), F32)],
-        [],
-        (mix, product),
-        tiles,
-    )[0]
-    grad, short_part = tiled(
-        backward_kernel,
-        [full_spec, front_spec, rows_spec, taps_spec, lines_spec, full_spec, padded_spec, front_spec],
-        [(*rows_spec, rows.shape, BF), ((1, HALO, LANES), lambda i: (i, 0, 0), (tiles, HALO, LANES), F32)],
         [line_rows, pltpu.VMEM((seqs, row_count, LANES), F32), line_rows, bands],
-        (cotangent, front, rows, short_w, lines_ahead, mixed, mix, later),
+        (cotangent, front, rows, short_w, medium_h, mixed, mix, product, later),
         tiles,
     )
 
-    pieces = ALONG_Z
-    packed = jnp.concatenate([filter_part, short_part.reshape(tiles * HALO, LANES)], axis=0)
-    depth = packed.shape[0] // pieces
-    piece = (depth, LANES)
-    peers = 2 * (lax.axis_size("ctx") // pieces)
-    sums = pl.pallas_call(
-        reduce_kernel,
-        out_shape=jax.ShapeDtypeStruct((pieces, *piece), F32),
-        in_specs=[pl.BlockSpec(memory_space=pltpu.VMEM)],
-        out_specs=pl.BlockSpec(memory_space=pltpu.VMEM),
+    seq_total = seqs * lax.axis_size("dp")
+    length_total = row_count * lax.axis_size("ctx")
+    scales = (
+        1.0 / math.sqrt(seq_total * length_total * (LANES // groups)),
+        1.0 / math.sqrt(seq_total * length_total),
+    )
+    sum_rows = groups_here + tiles * HALO
+    peers = 2 * (lax.axis_size("ctx") // ALONG_Z)
+    piece = (sum_rows // peers, LANES)
+    filter_grad, short_grad = pl.pallas_call(
+        functools.partial(reduce_kernel, ALONG_Z, scales),
+        out_shape=[jax.ShapeDtypeStruct((groups_here, taps), F32), jax.ShapeDtypeStruct(short_w.shape, F32)],
+        in_specs=[pl.BlockSpec(memory_space=pltpu.VMEM)] * 2,
+        out_specs=[pl.BlockSpec(memory_space=pltpu.VMEM)] * 2,
         scratch_shapes=[
-            pltpu.VMEM((pieces, *piece), F32), pltpu.VMEM(piece, F32),
-            pltpu.VMEM((peers, *piece), F32), pltpu.VMEM(piece, F32),
+            pltpu.VMEM((sum_rows, LANES), F32),
+            pltpu.VMEM((peers, *piece), F32),
+            pltpu.VMEM(piece, F32),
+            pltpu.VMEM((ALONG_Z, *piece), F32),
+            pltpu.VMEM(piece, F32),
+            pltpu.VMEM((sum_rows, LANES), F32),
         ]
         + [pltpu.SemaphoreType.DMA((8,))] * 6,
         compiler_params=pltpu.CompilerParams(collective_id=1, has_side_effects=True),
-    )(packed.reshape(pieces, *piece)).reshape(packed.shape)
-
-    seq_total = seqs * lax.axis_size("dp")
-    length_total = row_count * lax.axis_size("ctx")
-    filter_grad = sums[:groups_here, ::-1] / math.sqrt(seq_total * length_total * (LANES // groups))
-    streams = sums[groups_here:].reshape(tiles, HALO, LANES)[:, : 3 * short_w.shape[1]]
-    short_sum = jnp.swapaxes(streams, 0, 1).reshape(3, short_w.shape[1], chans)
-    short_grad = short_sum / math.sqrt(seq_total * length_total)
+    )(filter_part, short_part)
     return (block_out, jnp.swapaxes(grad, 1, 2), filter_grad, short_grad)
 
 

time: 178 us -> 170 us (0.955)
  Pallas kernels: 162 us -> 159 us
  other arithmetic: 2.71 us -> 0 us
  local copies, waits for them, and re-layouts: 12 us -> 9.36 us
    pallas_call x1, Pallas kernels: 118 us -> 123 us  [exchange(): pl.pallas_call(functools.partial(exchange_kernel, ALONG_Z), out_shape=[sh...]
    pallas_call x3 -> x1, Pallas kernels: 20.9 us -> 16.6 us  [tiled(): pl.pallas_call(kernel, grid=(tiles,), in_specs=[pl.BlockSpec(block, index...]
    pallas_call x1, Pallas kernels: 22.8 us -> 19.7 us  [shards(): pl.pallas_call(functools.partial(reduce_kernel, ALONG_Z, scales), out_sha...]
where the time goes in v4:
time: 170 us
  Pallas kernels  159 us (94%)
  local copies, waits for them, and re-layouts  9.36 us (6%)
    pallas_call x1, Pallas kernels, exchange(): pl.pallas_call(functools.partial(exchange_kernel, ALONG_Z), out_shape=[sh...  123 us
    pallas_call x1, Pallas kernels, shards(): pl.pallas_call(functools.partial(reduce_kernel, ALONG_Z, scales), out_sha...  19.7 us
    pallas_call x1, Pallas kernels, tiled(): pl.pallas_call(kernel, grid=(tiles,), in_specs=[pl.BlockSpec(block, index...  16.6 us
    unnamed x27, local copies, waits for them, and re-layouts  9.36 us

profile of v4, /device:TPU:1, one launch (start us, length us, event | category | flops | bytes accessed | tf_op | source)
XLA Modules:
  0.0 169.6 jit_solution(16466915840643795311)
XLA Ops:
  0.6 0.0 copy-start.6
  0.6 0.0 copy-start.8
  0.7 123.2 %shard_map.84 = (bf16[2,256,1024]{2,1,0:T(8,128)(2,1)}, bf16[2,256,1024]{2,1,0:T(8,128)(2,1)}, f32[2,256,1024]{2,1,0:T(8,128)}, bf16[2,384,1024]{2,1,0:T(8,128)(...) custom-call(bf16[128,1024]{1,0:T(8,128)(2,1)} %w_ref.1, ...), custom_call_target="tpu_custom_call" | custom-call | flops 8589934592 | bytes 4194304 | tf_op jit(solution)/shard_map/pallas_call | solution.py:602
  123.8 0.0 copy-done.6
  123.8 0.0 copy-done.8
  123.9 0.0 copy-start
  123.9 1.4 copy-done
  125.3 0.0 copy-start.1
  125.3 1.4 copy-done.1
  126.7 1.2 copy-done.2
  127.9 0.9 copy-done.3
  128.8 0.9 copy-done.4
  129.8 16.6 %shard_map.85 = (bf16[2,3,256,1024]{3,2,1,0:T(8,128)(2,1)}, f32[8,16,128]{2,1,0:T(8,128)S(1)}, f32[64,128]{1,0:T(8,128)S(1)}) custom-call(bf16[2,256,1024]{2,1,0:T(8,128)(2,1)S(1)} %copy-done.2, bf16[2,3,16,1024]{3,2,1,0:T(8,128)(2,1)S(1)} %copy-done.3, bf16[2,3,256,1024]{3,2,1,0:T(8,128)(2,1)} %bitcast.3, f32[3,3,1024]{2,1,0:T(4,128)S(1)} %copy-done.6, ...), custom_call_target="tpu_custom_call" | custom-call | bytes 9883648 | tf_op jit(solution)/shard_map/pallas_call | solution.py:641
  146.4 0.6 copy-done.5
  147.0 0.6 copy-done.7
  147.6 19.7 %shard_map.86 = (f32[64,128]{1,0:T(8,128)}, f32[3,3,1024]{2,1,0:T(4,128)}) custom-call(f32[64,128]{1,0:T(8,128)} %copy-done.7, f32[8,16,128]{2,1,0:T(8,128)} %copy-done.5), custom_call_target="tpu_custom_call" | custom-call | tf_op jit(solution)/shard_map/pallas_call | solution.py:697
  167.3 0.0 copy-start.11
  167.3 0.0 copy-start.10
  167.3 0.0 copy-done.9
  167.4 1.0 copy.12
  168.3 0.0 copy-done.11
  168.3 0.6 copy.13
  168.9 0.0 copy-done.10
  168.9 0.6 copy.14
  (6 shorter events, 0.0 us)
Async XLA Ops:
  0.6 123.2 %copy-start.6 = (f32[3,3,1024]{2,1,0:T(4,128)S(1)}, f32[3,3,1024]{2,1,0:T(4,128)}, u32[]{:S(2)}) copy-start(f32[3,3,1024]{2,1,0:T(4,128)} %taps_ref.3) | copy-start | bytes 110596
  0.6 123.2 %copy-start.8 = (bf16[64,128]{1,0:T(8,128)(2,1)S(1)}, bf16[64,128]{1,0:T(8,128)(2,1)}, u32[]{:S(2)}) copy-start(bf16[64,128]{1,0:T(8,128)(2,1)} %filters_ref.3) | copy-start | bytes 49156
  123.9 1.4 copy-start
  125.3 1.4 copy-start.1
  126.7 1.2 copy-start.2
  127.9 0.9 copy-start.3
  128.8 0.9 copy-start.4
  129.8 37.6 %copy-start.9 = (bf16[2,256,1024]{2,1,0:T(8,128)(2,1)S(1)}, bf16[2,256,1024]{2,1,0:T(8,128)(2,1)}, u32[]{:S(2)}) copy-start(bf16[2,256,1024]{2,1,0:T(8,128)(2,1)} %get-tuple-element.32) | copy-start | bytes 3145732
  146.4 0.6 copy-start.5
  147.0 0.6 copy-start.7
  167.3 1.0 copy-start.11
  167.3 1.6 copy-start.10

commit v5 on v4

--- a/solution.py
+++ b/solution.py
@@ -12,7 +12,8 @@
 F32 = jnp.float32
 LANES = 128
 BLOCK = 128
-HALO = 16
+HALO = 8
+SUM_ROWS = 16
 MESH = pl.DeviceIdType.MESH
 ALONG_Z = 8
 
@@ -441,23 +442,20 @@
         x_start(3)
 
     plan = []
-    for u in range(along_z + 2):
-        if 3 <= u < along_z:
-            plan.append((z_turn, u))
-        if 0 <= u - 1 < along_z and u > 0:
-            plan.append((y_turn, u - 1))
-        if 0 <= u - 2 < along_z and u > 1:
-            plan.append((far_turn, u - 2))
-        if u == min(3, along_z):
-            plan.append((second_half,))
-        if u == min(5, along_z + 1):
-            plan.append((x_turn, 0))
-        if u == min(6, along_z + 1):
+    for u in range(along_z):
+        plan += [(z_turn, u)] if u >= 3 else []
+        plan += [(y_turn, u - 3)] if u >= 3 else []
+        plan += [(far_turn, u - 4)] if u >= 4 else []
+    plan.insert(min(len(plan), 9), (x_turn, 0))
+    plan.insert(min(len(plan), 13), (second_half,))
+    for u in range(max(along_z - 3, 0), along_z):
+        plan += [(y_turn, u), (far_turn, u - 1)] if u > 0 else [(y_turn, u)]
+        if u == along_z - 3:
             plan.append((x_turn, 1))
-        if u == along_z:
-            plan.append((x_turn, 2))
+    plan += [(far_turn, along_z - 1), (x_turn, 2)]
     if along_z < 8:
-        plan = [p for p in plan if p[0] is not x_turn] + [(x_turn, c) for c in range(3)]
+        plan = [(second_half,)] + [(x_turn, c) for c in range(3)]
+        plan += [(y_turn, u) for u in range(along_z)] + [(far_turn, u) for u in range(along_z)]
     for what, *which in plan:
         what(*which)
     for kind, step_y in enumerate((0, -1, 1, 2)):
@@ -556,6 +554,11 @@
             grad_ref[s, here, :] = found
             mix_ref[s, here, :] = (found.astype(F32) * queries[s, here, :]).astype(BF)
 
+    def low_bands(i, carry):
+        band_rows(ahead_lines(lines_of(filters_ref, i)), low_band.at[i], HALO)
+        return carry
+
+    lax.fori_loop(0, tiles, low_bands, 0)
     wait_sum(8, from_right.at[first, :])
     for n in range(2):
         wait_sum(4 + n, piece(from_left, 0, n))
@@ -567,8 +570,7 @@
     finish(1)
 
     def heads(i, carry):
-        band_rows(ahead_lines(lines_of(filters_ref, i)), low_band, HALO)
-        low = jnp.dot(low_band[...], window_pair(mix_ref, 0, lanes_of(i)), preferred_element_type=F32)
+        low = jnp.dot(low_band[i], window_pair(mix_ref, 0, lanes_of(i)), preferred_element_type=F32)
         pulled = own_group(low, groups, HALO)
         for s in range(seqs):
             here = pulled[:, s * LANES : (s + 1) * LANES]
@@ -622,7 +624,7 @@
             pltpu.VMEM(edge, BF),
             pltpu.VMEM((row_count + HALO, LANES), F32),
             pltpu.VMEM((tiles, groups * BLOCK, 2 * BLOCK), BF),
-            pltpu.VMEM((groups * HALO, 2 * BLOCK), BF),
+            pltpu.VMEM((tiles, groups * HALO, 2 * BLOCK), BF),
         ]
         + [dma((ALONG_Z,))] * 8
         + [dma((4 * ALONG_Z,))] * 2
@@ -646,7 +648,7 @@
         out_shape=[jax.ShapeDtypeStruct(shape, kind) for _, _, shape, kind in outs],
         scratch_shapes=scratch,
         cost_estimate=pl.CostEstimate(flops=flops, bytes_accessed=read, transcendentals=0),
-        compiler_params=pltpu.CompilerParams(vmem_limit_bytes=48 << 20),
+        compiler_params=pltpu.CompilerParams(vmem_limit_bytes=60 << 20),
     )(*arrays)
 
 
@@ -677,7 +679,7 @@
         [full_spec, front_spec, rows_spec, taps_spec, filters_spec, full_spec, padded_spec, padded_spec, front_spec],
         [
             (*rows_spec, rows.shape, BF),
-            ((1, HALO, LANES), lambda i: (i, 0, 0), (tiles, HALO, LANES), F32),
+            ((1, SUM_ROWS, LANES), lambda i: (i, 0, 0), (tiles, SUM_ROWS, LANES), F32),
             ((groups, LANES), lambda i: (i, 0), (groups_here, taps), F32),
         ],
         [line_rows, pltpu.VMEM((seqs, row_count, LANES), F32), line_rows, bands],
@@ -691,7 +693,7 @@
         1.0 / math.sqrt(seq_total * length_total * (LANES // groups)),
         1.0 / math.sqrt(seq_total * length_total),
     )
-    sum_rows = groups_here + tiles * HALO
+    sum_rows = groups_here + tiles * SUM_ROWS
     peers = 2 * (lax.axis_size("ctx") // ALONG_Z)
     piece = (sum_rows // peers, LANES)
     filter_grad, short_grad = pl.pallas_call(

time: 170 us -> 157 us (0.924)
  local copies, waits for them, and re-layouts: 9.36 us -> 2.22 us
  Pallas kernels: 159 us -> 154 us
    unnamed x27 -> x9, local copies, waits for them, and re-layouts: 9.36 us -> 2.22 us
    pallas_call x1, Pallas kernels: 123 us -> 116 us  [exchange(): pl.pallas_call(functools.partial(exchange_kernel, ALONG_Z), out_shape=[sh...]
    pallas_call x1, Pallas kernels: 19.7 us -> 21.7 us  [shards(): pl.pallas_call(functools.partial(reduce_kernel, ALONG_Z, scales), out_sha...]
where the time goes in v5:
time: 157 us
  Pallas kernels  154 us (98%)
  local copies, waits for them, and re-layouts  2.22 us (1%)
    pallas_call x1, Pallas kernels, exchange(): pl.pallas_call(functools.partial(exchange_kernel, ALONG_Z), out_shape=[sh...  116 us
    pallas_call x1, Pallas kernels, shards(): pl.pallas_call(functools.partial(reduce_kernel, ALONG_Z, scales), out_sha...  21.7 us
    pallas_call x1, Pallas kernels, tiled(): pl.pallas_call(kernel, grid=(tiles,), in_specs=[pl.BlockSpec(block, index...  16 us

profile of v5, /device:TPU:1, one launch (start us, length us, event | category | flops | bytes accessed | tf_op | source)
XLA Modules:
  0.0 156.8 jit_solution(11517014381146827388)
XLA Ops:
  0.6 116.1 %shard_map.84 = (bf16[2,256,1024]{2,1,0:T(8,128)(2,1)}, bf16[2,256,1024]{2,1,0:T(8,128)(2,1)}, f32[2,256,1024]{2,1,0:T(8,128)}, bf16[2,384,1024]{2,1,0:T(8,128)(...) custom-call(bf16[128,1024]{1,0:T(8,128)(2,1)} %w_ref.1, ...), custom_call_target="tpu_custom_call" | custom-call | flops 8589934592 | bytes 4194304 | tf_op jit(solution)/shard_map/pallas_call | solution.py:604
  116.8 0.0 copy-start
  116.8 16.0 %shard_map.85 = (bf16[2,3,256,1024]{3,2,1,0:T(8,128)(2,1)}, f32[8,16,128]{2,1,0:T(8,128)}, f32[64,128]{1,0:T(8,128)}) custom-call(bf16[2,256,1024]{2,1,0:T(8,128)(2,1)} %get-tuple-element.17.cotangent_ref, bf16[2,3,8,1024]{3,2,1,0:T(8,128)(2,1)} %get-tuple-element.18.front_ref, bf16[2,3,256,1024]{3,2,1,0:T(8,128)(2,1)} %bitcast.3, f32[3,3,1024]{2,1,0:T(4,128)} %taps_ref.3, ...), custom_call_target="tpu_custom_call" | custom-call | bytes 9687040 | tf_op jit(solution)/shard_map/pallas_call | solution.py:643
  132.8 21.7 %shard_map.86 = (f32[64,128]{1,0:T(8,128)}, f32[3,3,1024]{2,1,0:T(4,128)}) custom-call(f32[64,128]{1,0:T(8,128)} %get-tuple-element.24.filter_ref, f32[8,16,128]{2,1,0:T(8,128)} %get-tuple-element.25.short_ref), custom_call_target="tpu_custom_call" | custom-call | tf_op jit(solution)/shard_map/pallas_call | solution.py:699
  154.6 0.0 copy-start.2
  154.6 0.0 copy-start.1
  154.6 0.0 copy-done
  154.6 1.0 copy.12
  155.6 0.0 copy-done.2
  155.6 0.6 copy.13
  156.2 0.0 copy-done.1
  156.2 0.6 copy.14
Async XLA Ops:
  116.8 37.8 %copy-start = (bf16[2,256,1024]{2,1,0:T(8,128)(2,1)S(1)}, bf16[2,256,1024]{2,1,0:T(8,128)(2,1)}, u32[]{:S(2)}) copy-start(bf16[2,256,1024]{2,1,0:T(8,128)(2,1)} %get-tuple-element.32) | copy-start | bytes 3145732
  154.6 1.0 copy-start.2
  154.6 1.6 %copy-start.1 = (f32[3,3,1024]{2,1,0:T(4,128)S(1)}, f32[3,3,1024]{2,1,0:T(4,128)}, u32[]{:S(2)}) copy-start(f32[3,3,1024]{2,1,0:T(4,128)} %get-tuple-element.35) | copy-start | bytes 110596

commit v6 on v5

--- a/solution.py
+++ b/solution.py
@@ -70,22 +70,15 @@
     )
 
 
-def filter_sums(mix_ref, product_ref, sums_ref):
-    seqs, row_count = product_ref.shape[0], product_ref.shape[1] - BLOCK
-    groups = sums_ref.shape[0]
+def filter_sums(grads, windows, groups):
     rows = lax.broadcasted_iota(jnp.int32, (2 * BLOCK, 2 * BLOCK), 0)
     columns = lax.broadcasted_iota(jnp.int32, (2 * BLOCK, 2 * BLOCK), 1)
     upturn = (rows + columns == 2 * BLOCK - 1).astype(BF)
-    parts, wins = [], []
-    for s in range(seqs):
-        for b in range(row_count // BLOCK):
-            parts.append(mix_ref[s, b * BLOCK : (b + 1) * BLOCK, :])
-            wins.append(product_ref[s, b * BLOCK : (b + 2) * BLOCK, :])
-    grads = jnp.concatenate(parts, axis=1)
-    windows = jnp.dot(upturn, jnp.concatenate(wins, axis=1), preferred_element_type=F32).astype(BF)
+    windows = jnp.dot(upturn, windows, preferred_element_type=F32).astype(BF)
     owner = group_of_lane(grads.shape, groups)
+    wide = grads.astype(F32)
     stacked = jnp.concatenate(
-        [jnp.where(owner == g, grads.astype(F32), 0.0).astype(BF) for g in range(groups)], axis=0
+        [jnp.where(owner == g, wide, 0.0).astype(BF) for g in range(groups)], axis=0
     )
     lags = lax.dot_general(
         stacked, windows, (((1,), (1,)), ((), ())), preferred_element_type=F32
@@ -94,17 +87,16 @@
     for g in range(groups):
         turned = pltpu.roll(lags[g * BLOCK : (g + 1) * BLOCK], 0, 1, stride=1, stride_axis=0)
         found.append(jnp.sum(turned, axis=0, keepdims=True))
-    sums_ref[...] = pltpu.roll(jnp.concatenate(found, axis=0), BLOCK + 1, 1)[:, :BLOCK]
+    return pltpu.roll(jnp.concatenate(found, axis=0), BLOCK + 1, 1)[:, :BLOCK]
 
 
 def backward_kernel(
     cotangent_ref, front_ref, rows_ref, taps_ref, filters_ref, mixed_ref,
-    padded_ref, product_ref, next_ref, grad_ref, short_ref, sums_ref, scratch, pulled, later, band,
+    padded_ref, next_ref, grad_ref, short_ref, scratch, pulled, later, band,
 ):
     seqs, row_count = rows_ref.shape[0], rows_ref.shape[2]
-    groups = sums_ref.shape[0]
+    groups = band.shape[0] // BLOCK
     taps = taps_ref.shape[1]
-    filter_sums(padded_ref, product_ref, sums_ref)
     first = pl.multiple_of(pl.program_id(0) * groups, groups)
     band_rows(ahead_lines(filters_ref[pl.ds(first, groups), :]), band)
     for b in range(row_count // BLOCK):
@@ -233,8 +225,8 @@
 
 def exchange_kernel(
     along_z, w_ref, rows_ref, taps_ref, filters_ref, cotangent_ref,
-    out_ref, grad_ref, mixed_ref, product_ref, mix_ref, front_ref, later_ref,
-    whole, gated, gathered, turned, queries, to_a, to_b, from_a, from_b,
+    out_ref, grad_ref, mixed_ref, mix_ref, front_ref, later_ref, sums_ref,
+    product_ref, whole, gated, gathered, turned, queries, to_a, to_b, from_a, from_b,
     to_right, to_left, from_left, from_right, kept_right, kept_left, own, head,
     scratch, band, low_band,
     z_send, z_recv, up_send, up_recv, down_send, down_recv, far_send, far_recv,
@@ -244,6 +236,7 @@
     size, ring = lax.axis_size("ctx"), lax.axis_size("grp")
     lines = size // along_z
     y, z = ctx // along_z, ctx % along_z
+    edge = jnp.where((z + 1) % along_z < 2, 1, 0)
     part = w_ref.shape[0] // 2
     total, chans = gated.shape
     half = total // 2
@@ -333,13 +326,14 @@
     def y_turn(u):
         behind, ahead = block(-1, steps[u], core), block(1, steps[u], core)
         arrive(behind, up_send.at[u], up_recv.at[u], at_y(1))
-        if u % 2 == 0:
-            go(behind, behind, far_send.at[u], far_recv.at[u], at_y(1))
         hand_over(1, -1, u)
         arrive(ahead, down_send.at[u], down_recv.at[u], at_y(-1))
-        if u % 2 == 1:
-            go(ahead, ahead, far_send.at[u], far_recv.at[u], at_y(-1))
         hand_over(2, 1, u)
+        up = 1 if u % 2 == 0 else -1
+        if u % 4 == 0:
+            up = 1 - 2 * edge
+        onward = block(-up, steps[u], core)
+        go(onward, onward, far_send.at[u], far_recv.at[u], at_y(up))
 
     def far_turn(u):
         arrive(block(2, steps[u], core), far_send.at[u], far_recv.at[u], at_y(1))
@@ -564,6 +558,24 @@
         wait_sum(4 + n, piece(from_left, 0, n))
     finish(0)
     halo(2, mix_ref.at[:, 0:BLOCK, :], mix_ref.at[:, row_count:, :], at_ctx(-1))
+
+    def block_sums(i, b):
+        grads = [mix_ref[s, b * BLOCK : (b + 1) * BLOCK, lanes_of(i)] for s in range(seqs)]
+        windows = window_pair(product_ref, b * BLOCK, lanes_of(i))
+        return filter_sums(jnp.concatenate(grads, axis=1), windows, groups)
+
+    def sums_of(i):
+        return pl.ds(pl.multiple_of(i * groups, groups), groups)
+
+    def first_sums(i, carry):
+        sums_ref[sums_of(i), :] = block_sums(i, 0)
+        return carry
+
+    def second_sums(i, carry):
+        sums_ref[sums_of(i), :] += block_sums(i, 1)
+        return carry
+
+    lax.fori_loop(0, tiles, first_sums, 0)
     wait_sum(9, from_left.at[second, :])
     for n in range(2):
         wait_sum(6 + n, piece(from_right, half, n))
@@ -583,6 +595,7 @@
 
     lax.fori_loop(0, tiles, heads, 0)
     halo(3, head, later_ref, at_ctx(-1))
+    lax.fori_loop(0, tiles, second_sums, 0)
     halo_wait(2, mix_ref.at[:, row_count:, :], at_ctx(-1), size - 1)
     halo_wait(3, later_ref, at_ctx(-1), size - 1)
     for sent in started:
@@ -605,11 +618,12 @@
         functools.partial(exchange_kernel, ALONG_Z),
         out_shape=[
             shape(grad_out.shape, BF), shape(grad_out.shape, BF), shape(grad_out.shape, F32),
-            shape(padded, BF), shape(padded, BF), shape(edge, BF), shape(edge, BF),
+            shape(padded, BF), shape(edge, BF), shape(edge, BF), shape(medium_h.shape, F32),
         ],
         in_specs=[pl.BlockSpec(memory_space=pltpu.VMEM)] * 5,
         out_specs=[pl.BlockSpec(memory_space=pltpu.VMEM)] * 7,
         scratch_shapes=[
+            pltpu.VMEM(padded, BF),
             pltpu.VMEM((depth, chans), BF),
             pltpu.VMEM((total, chans), BF),
             pltpu.VMEM((3, total, chans), BF),
@@ -671,19 +685,18 @@
     padded_spec = ((seqs, row_count + BLOCK, LANES), lane3)
     bands = pltpu.VMEM((groups * BLOCK, 2 * BLOCK), BF)
 
-    block_out, cotangent, mixed, product, mix, front, later = exchange(
+    block_out, cotangent, mixed, mix, front, later, filter_part = exchange(
         out_w, rows, short_w, medium_h, grad_out
     )
-    grad, short_part, filter_part = tiled(
+    grad, short_part = tiled(
         backward_kernel,
-        [full_spec, front_spec, rows_spec, taps_spec, filters_spec, full_spec, padded_spec, padded_spec, front_spec],
+        [full_spec, front_spec, rows_spec, taps_spec, filters_spec, full_spec, padded_spec, front_spec],
         [
             (*rows_spec, rows.shape, BF),
             ((1, SUM_ROWS, LANES), lambda i: (i, 0, 0), (tiles, SUM_ROWS, LANES), F32),
-            ((groups, LANES), lambda i: (i, 0), (groups_here, taps), F32),
         ],
         [line_rows, pltpu.VMEM((seqs, row_count, LANES), F32), line_rows, bands],
-        (cotangent, front, rows, short_w, medium_h, mixed, mix, product, later),
+        (cotangent, front, rows, short_w, medium_h, mixed, mix, later),
         tiles,
     )
 

time: 157 us -> 155 us (0.987)
  Pallas kernels: 154 us -> 150 us
    pallas_call x1, Pallas kernels: 16 us -> 13.4 us  [tiled(): pl.pallas_call(kernel, grid=(tiles,), in_specs=[pl.BlockSpec(block, index...]
    pallas_call x1, Pallas kernels: 21.7 us -> 20 us  [shards(): pl.pallas_call(functools.partial(reduce_kernel, ALONG_Z, scales), out_sha...]
    unnamed x9 -> x5, local copies, waits for them, and re-layouts: 2.22 us -> 3.78 us
where the time goes in v6:
time: 155 us
  Pallas kernels  150 us (97%)
  local copies, waits for them, and re-layouts  3.78 us (2%)
    pallas_call x1, Pallas kernels, exchange(): pl.pallas_call(functools.partial(exchange_kernel, ALONG_Z), out_shape=[sh...  117 us
    pallas_call x1, Pallas kernels, shards(): pl.pallas_call(functools.partial(reduce_kernel, ALONG_Z, scales), out_sha...  20 us
    pallas_call x1, Pallas kernels, tiled(): pl.pallas_call(kernel, grid=(tiles,), in_specs=[pl.BlockSpec(block, index...  13.4 us
    unnamed x5, local copies, waits for them, and re-layouts  3.78 us

profile of v6, /device:TPU:1, one launch (start us, length us, event | category | flops | bytes accessed | tf_op | source)
XLA Modules:
  0.0 154.9 jit_solution(5377952361300874290)
XLA Ops:
  0.6 117.1 %shard_map.84 = (bf16[2,256,1024]{2,1,0:T(8,128)(2,1)}, bf16[2,256,1024]{2,1,0:T(8,128)(2,1)}, f32[2,256,1024]{2,1,0:T(8,128)}, bf16[2,384,1024]{2,1,0:T(8,128)(...) custom-call(bf16[128,1024]{1,0:T(8,128)(2,1)} %w_ref.1, ...), custom_call_target="tpu_custom_call" | custom-call | flops 8589934592 | bytes 4194304 | tf_op jit(solution)/shard_map/pallas_call | solution.py:617
  117.7 0.0 copy-start
  117.7 13.4 %shard_map.85 = (bf16[2,3,256,1024]{3,2,1,0:T(8,128)(2,1)}, f32[8,16,128]{2,1,0:T(8,128)}) custom-call(bf16[2,256,1024]{2,1,0:T(8,128)(2,1)} %get-tuple-element.16.cotangent_ref, bf16[2,3,8,1024]{3,2,1,0:T(8,128)(2,1)} %get-tuple-element.17.front_ref, bf16[2,3,256,1024]{3,2,1,0:T(8,128)(2,1)} %bitcast.3, f32[3,3,1024]{2,1,0:T(4,128)} %taps_ref.3, ...), custom_call_target="tpu_custom_call" | custom-call | bytes 8114176 | tf_op jit(solution)/shard_map/pallas_call | solution.py:657
  131.1 20.0 %shard_map.86 = (f32[64,128]{1,0:T(8,128)}, f32[3,3,1024]{2,1,0:T(4,128)}) custom-call(f32[64,128]{1,0:T(8,128)} %get-tuple-element.22.filter_ref, f32[8,16,128]{2,1,0:T(8,128)} %get-tuple-element.23.short_ref), custom_call_target="tpu_custom_call" | custom-call | tf_op jit(solution)/shard_map/pallas_call | solution.py:712
  151.2 0.0 copy-done
  151.2 1.0 copy.12
  152.1 1.4 copy.13
  153.5 1.4 copy.14
Async XLA Ops:
  117.7 33.5 %copy-start = (bf16[2,256,1024]{2,1,0:T(8,128)(2,1)S(1)}, bf16[2,256,1024]{2,1,0:T(8,128)(2,1)}, u32[]{:S(2)}) copy-start(bf16[2,256,1024]{2,1,0:T(8,128)(2,1)} %get-tuple-element.30) | copy-start | bytes 3145732

commit v7 on v6

--- a/solution.py
+++ b/solution.py
@@ -109,14 +109,14 @@
     sums = [None] * (3 * taps)
     for s in range(seqs):
         for stream in range(3):
+            fill(scratch.at[stream], front_ref[s, stream], rows_ref[s, stream])
+        for stream in range(3):
             if stream == 0:
                 grad = cotangent_ref[s].astype(F32) * mixed_ref[s]
             else:
                 other = 3 - stream
-                fill(scratch, front_ref[s, other], rows_ref[s, other])
-                grad = pulled[s] * feature(scratch, taps_ref, other, row_count)
+                grad = pulled[s] * feature(scratch.at[other], taps_ref, other, row_count)
             grad = grad.astype(BF).astype(F32)
-            fill(scratch, front_ref[s, stream], rows_ref[s, stream])
             later[0:row_count, :] = grad
             later[row_count : row_count + HALO, :] = next_ref[s, stream].astype(F32)
             total = None
@@ -124,7 +124,7 @@
                 term = taps_ref[stream, offset : offset + 1, :] * later[offset : offset + row_count, :]
                 total = term if total is None else total + term
                 at = HALO - offset
-                found = jnp.sum(grad * scratch[at : at + row_count, :], axis=0, keepdims=True)
+                found = jnp.sum(grad * scratch[stream, at : at + row_count, :], axis=0, keepdims=True)
                 row = stream * taps + offset
                 sums[row] = found if sums[row] is None else sums[row] + found
             grad_ref[s, stream] = total.astype(BF)
@@ -318,10 +318,22 @@
             if onward in steps and (u == 0 or steps[u] * direction > 0):
                 v = steps.index(onward)
                 go(mine, block(0, steps[u], core), z_send.at[v], z_recv.at[v], at_z(-direction))
-        go(mine, block(0, steps[u], core), up_send.at[u], up_recv.at[u], at_y(1))
+        upward = copy(mine, block(0, steps[u], core), up_send.at[u], up_recv.at[u], at_y(1))
+        started.append(upward)
+        if along_z >= 8 and 1 <= u <= 4:
+            pl.when(z != 0)(upward.start)
+            held.append(upward)
+        else:
+            upward.start()
         go(mine, block(0, steps[u], core), down_send.at[u], down_recv.at[u], at_y(-1))
         if u > 0:
             hand_over(0, 0, u)
+
+    held = []
+
+    def release():
+        for upward in held:
+            pl.when(z == 0)(upward.start)
 
     def y_turn(u):
         behind, ahead = block(-1, steps[u], core), block(1, steps[u], core)
@@ -447,6 +459,10 @@
         if u == along_z - 3:
             plan.append((x_turn, 1))
     plan += [(far_turn, along_z - 1), (x_turn, 2)]
+    if along_z >= 8:
+        plan.remove((z_turn, 5))
+        at = plan.index((y_turn, 1))
+        plan[at:at] = [(z_turn, 5), (release,)]
     if along_z < 8:
         plan = [(second_half,)] + [(x_turn, c) for c in range(3)]
         plan += [(y_turn, u) for u in range(along_z)] + [(far_turn, u) for u in range(along_z)]
@@ -695,7 +711,12 @@
             (*rows_spec, rows.shape, BF),
             ((1, SUM_ROWS, LANES), lambda i: (i, 0, 0), (tiles, SUM_ROWS, LANES), F32),
         ],
-        [line_rows, pltpu.VMEM((seqs, row_count, LANES), F32), line_rows, bands],
+        [
+            pltpu.VMEM((3, row_count + HALO, LANES), F32),
+            pltpu.VMEM((seqs, row_count, LANES), F32),
+            line_rows,
+            bands,
+        ],
         (cotangent, front, rows, short_w, medium_h, mixed, mix, later),
         tiles,
     )

time: 155 us -> 158 us (1.019)
  Pallas kernels: 150 us -> 153 us
    pallas_call x1, Pallas kernels: 117 us -> 121 us  [exchange(): pl.pallas_call(functools.partial(exchange_kernel, ALONG_Z), out_shape=[sh...]
where the time goes in v7:
time: 158 us; the launch traced here: 157 us
  Pallas kernels  153 us (97%)
  local copies, waits for them, and re-layouts  3.78 us (2%)
    pallas_call x1, Pallas kernels, exchange(): pl.pallas_call(functools.partial(exchange_kernel, ALONG_Z), out_shape=[sh...  121 us
    pallas_call x1, Pallas kernels, shards(): pl.pallas_call(functools.partial(reduce_kernel, ALONG_Z, scales), out_sha...  19.7 us
    pallas_call x1, Pallas kernels, tiled(): pl.pallas_call(kernel, grid=(tiles,), in_specs=[pl.BlockSpec(block, index...  12.3 us
    unnamed x5, local copies, waits for them, and re-layouts  3.78 us

profile of v7, /device:TPU:1, one launch (start us, length us, event | category | flops | bytes accessed | tf_op | source)
XLA Modules:
  0.0 157.2 jit_solution(5106817484615598945)
XLA Ops:
  0.6 120.7 %shard_map.84 = (bf16[2,256,1024]{2,1,0:T(8,128)(2,1)}, bf16[2,256,1024]{2,1,0:T(8,128)(2,1)}, f32[2,256,1024]{2,1,0:T(8,128)}, bf16[2,384,1024]{2,1,0:T(8,128)(...) custom-call(bf16[128,1024]{1,0:T(8,128)(2,1)} %w_ref.1, ...), custom_call_target="tpu_custom_call" | custom-call | flops 8589934592 | bytes 4194304 | tf_op jit(solution)/shard_map/pallas_call | solution.py:633
  121.3 0.0 copy-start
  121.4 12.3 %shard_map.85 = (bf16[2,3,256,1024]{3,2,1,0:T(8,128)(2,1)}, f32[8,16,128]{2,1,0:T(8,128)}) custom-call(bf16[2,256,1024]{2,1,0:T(8,128)(2,1)} %get-tuple-element.16.cotangent_ref, bf16[2,3,8,1024]{3,2,1,0:T(8,128)(2,1)} %get-tuple-element.17.front_ref, bf16[2,3,256,1024]{3,2,1,0:T(8,128)(2,1)} %bitcast.3, f32[3,3,1024]{2,1,0:T(4,128)} %taps_ref.3, ...), custom_call_target="tpu_custom_call" | custom-call | bytes 8114176 | tf_op jit(solution)/shard_map/pallas_call | solution.py:673
  133.7 19.7 %shard_map.86 = (f32[64,128]{1,0:T(8,128)}, f32[3,3,1024]{2,1,0:T(4,128)}) custom-call(f32[64,128]{1,0:T(8,128)} %get-tuple-element.22.filter_ref, f32[8,16,128]{2,1,0:T(8,128)} %get-tuple-element.23.short_ref), custom_call_target="tpu_custom_call" | custom-call | tf_op jit(solution)/shard_map/pallas_call | solution.py:733
  153.4 0.0 copy-done
  153.4 1.0 copy.12
  154.4 1.4 copy.13
  155.8 1.4 copy.14
Async XLA Ops:
  121.3 32.1 %copy-start = (bf16[2,256,1024]{2,1,0:T(8,128)(2,1)S(1)}, bf16[2,256,1024]{2,1,0:T(8,128)(2,1)}, u32[]{:S(2)}) copy-start(bf16[2,256,1024]{2,1,0:T(8,128)(2,1)} %get-tuple-element.30) | copy-start | bytes 3145732
